TPU v7x, 256 devices: a whole 4x4x8 slice. The times are simulated.
256 devices in a mesh: obs: 32 (over z, x_hi, core), ind: 8 (over y, x_lo).
Axes of the slice: x: 4 (x_hi: 2, x_lo: 2; x = x_hi * 2 + x_lo), y: 4, z: 8, core: 2. Of those that a mesh axis runs over, the one named last changes fastest.
Arguments:
- obs_coords: float32 [2, 131072], P(None, 'obs'), may hold values from 0 to 1
- obs_codes: int32 [131072], P('obs'), may hold values from 0 to 47
- route_plan: int32 [32, 32], replicated, may hold values from 0 to 1, as said below
- inducing_coords: float32 [2, 8192], P(None, 'ind'), may hold values from 0 to 1
- inducing_bands: int32 [8192], P('ind'), may hold values from 0 to 5
- band_mix: float32 [6, 6], replicated, may hold values from -2.4 to 2.4
- lengthscales: float32 [2], replicated, may hold values from 0.04 to 0.1
- class_scales: float32 [8], replicated, may hold values from 0.5 to 2
- prior_factor: bfloat16 [8192, 1024], P(('ind', 'obs')), may hold values from -0.046875 to 0.046875
- variational_chol: bfloat16 [8192, 1024], P(('ind', 'obs')), may hold values from -1 to 1, as said below
- variational_mean: bfloat16 [8, 8192], P(None, 'ind'), may hold values from -6 to 6
Outputs:
- class_probs: float32 [8, 65536], P(None, 'obs')
- grad_chol: float32 [8192, 1024], P(('ind', 'obs'))
- grad_mean: float32 [8, 8192], P(None, 'ind')
Inputs may be any that keep to these rules, and one draw needn't show every extreme that they name: `route_plan`: entry [s, d] is the number of 128-row blocks that reader s hands to device d; every column sums to 16; a reader's blocks go out in order of destination from the front of its buffer. `variational_chol`: each block's rows are lower triangular within the block, with diagonal entries of 0.3 to 1.
All inputs are finite; a program needn't handle non-finite values.
Results may differ from a plain program's by a relative error of at most 0.014.
Values may be sent and summed in bfloat16 or wider, within the bound.
A program may use at most 64 MiB of HBM per device.

v0:
```python
import jax
import jax.numpy as jnp
from jax import lax
from jax.sharding import PartitionSpec as P

C = 8
NB = 6
ROWS_DEV = 2048


precise = lax.Precision.HIGHEST


def cross_cov(coords, band_ids, centers, center_bands, lengthscales, coupling):
    delta_t = (coords[0][:, None] - centers[0][None, :]) / lengthscales[0]
    delta_w = (coords[1][:, None] - centers[1][None, :]) / lengthscales[1]
    kinds = jnp.arange(NB, dtype=jnp.int32)
    row_hot = (band_ids[:, None] == kinds[None, :]).astype(jnp.float32)
    col_hot = (center_bands[:, None] == kinds[None, :]).astype(jnp.float32)
    mixing = jnp.dot(jnp.dot(row_hot, coupling, precision=precise), col_hot.T, precision=precise)
    return (jnp.exp(-0.5 * (delta_t * delta_t + delta_w * delta_w)) * mixing).astype(jnp.bfloat16)


def likelihood(mean_sum, variance, class_scales):
    logits = mean_sum + 0.5 * class_scales[:, None] * variance[None, :]
    weights = jnp.exp(logits)
    chances = weights / jnp.sum(weights, axis=0, keepdims=True)
    var_slope = -0.5 * jnp.sum(chances * class_scales[:, None], axis=0)
    return (chances, var_slope)


def body(
    obs_coords,
    obs_codes,
    route_plan,
    inducing_coords,
    inducing_bands,
    band_mix,
    lengthscales,
    class_scales,
    prior_factor,
    variational_chol,
    variational_mean,
):
    devices = lax.axis_size("obs")
    my_index = lax.axis_index("obs")
    slot_rows = 128
    blocks = route_plan * slot_rows
    send_start = jnp.cumsum(blocks, axis=1) - blocks
    recv_start = jnp.cumsum(blocks, axis=0) - blocks
    my_sends = lax.dynamic_index_in_dim(send_start, my_index, 0, keepdims=False)
    my_recvs = lax.dynamic_index_in_dim(recv_start, my_index, 1, keepdims=False)
    stacked = jnp.concatenate([obs_coords, obs_codes.astype(jnp.float32)[None, :]], axis=0)
    padded = jnp.concatenate([stacked, jnp.zeros((3, slot_rows), jnp.float32)], axis=1)
    outgoing = jax.vmap(lambda offset: lax.dynamic_slice_in_dim(padded, offset, slot_rows, 1))(
        my_sends
    )
    incoming = lax.all_to_all(outgoing, "obs", split_axis=0, concat_axis=0, tiled=True)
    position = jnp.arange(ROWS_DEV, dtype=jnp.int32)
    sources = jnp.arange(devices, dtype=jnp.int32)
    source = jnp.sum((my_recvs[None, :] <= position[:, None]).astype(jnp.int32), axis=1) - 1
    pick = (source[:, None] == sources[None, :]).astype(jnp.int32)
    begin_row = jnp.sum(pick * my_recvs[None, :], axis=1)
    arrived = incoming[source, :, position - begin_row].T
    coords = arrived[0:2]
    code_ids = arrived[2].astype(jnp.int32)
    band_ids = code_ids % NB
    labels = code_ids // NB
    coupling = jnp.eye(NB, dtype=jnp.float32) + jnp.dot(band_mix, band_mix.T, precision=precise)
    kinds = jnp.arange(NB, dtype=jnp.int32)
    row_hot = (band_ids[:, None] == kinds[None, :]).astype(jnp.float32)
    self_cov = jnp.sum(row_hot * jnp.dot(row_hot, coupling, precision=precise), axis=1)
    kernel_rows = cross_cov(
        coords, band_ids, inducing_coords, inducing_bands, lengthscales, coupling
    )
    prior_block, chol_block = (
        lax.all_gather(prior_factor, "obs", axis=0, tiled=True),
        lax.all_gather(variational_chol, "obs", axis=0, tiled=True),
    )
    whitened = jnp.dot(kernel_rows, prior_block, preferred_element_type=jnp.float32)
    whitened_bf = whitened.astype(jnp.bfloat16)
    covariant = jnp.dot(whitened_bf, chol_block, preferred_element_type=jnp.float32)
    mean_part = lax.dot_general(
        variational_mean, whitened_bf, (((1,), (1,)), ((), ())), preferred_element_type=jnp.float32
    )
    var_part = (jnp.sum(covariant * covariant, axis=1) - jnp.sum(whitened * whitened, axis=1))[
        None, :
    ]
    mean_sum, var_sum = lax.psum((mean_part, var_part), "ind")
    chances, var_slope = likelihood(mean_sum, self_cov + var_sum[0], class_scales)
    classes = jnp.arange(C, dtype=jnp.int32)
    mean_slope = ((labels[None, :] == classes[:, None]).astype(jnp.float32) - chances).astype(
        jnp.bfloat16
    )
    heavy = (2.0 * var_slope[:, None] * covariant).astype(jnp.bfloat16)
    piece_rows = variational_chol.shape[0]
    full_width = variational_chol.shape[1]
    column_ids = jnp.arange(full_width, dtype=jnp.int32)
    own_rows = my_index * piece_rows + jnp.arange(piece_rows, dtype=jnp.int32)[:, None]
    term = lax.dot_general(
        whitened_bf, heavy, (((0,), (0,)), ((), ())), preferred_element_type=jnp.float32
    )
    row_ids = jnp.arange(lax.axis_size("obs") * piece_rows, dtype=jnp.int32)[:, None]
    data_term = lax.psum_scatter(
        jnp.where(column_ids[None, :] <= row_ids, term, 0.0).astype(jnp.bfloat16),
        "obs",
        scatter_dimension=0,
        tiled=True,
    ).astype(jnp.float32)
    on_diag = column_ids[None, :] == own_rows
    own_chol = variational_chol.astype(jnp.float32)
    diagonal = jnp.sum(jnp.where(on_diag, own_chol, 0.0), axis=1, keepdims=True)
    grad_chol = data_term - own_chol + jnp.where(on_diag, 1.0 / diagonal, 0.0)
    mean_term = lax.dot_general(
        mean_slope, whitened_bf, (((1,), (0,)), ((), ())), preferred_element_type=jnp.float32
    )
    grad_mean = lax.psum(mean_term, "obs") - variational_mean.astype(jnp.float32)
    return (chances, grad_chol, grad_mean)


def solution(mesh):
    placed = (
        P(None, "obs"),
        P("obs"),
        P(),
        P(None, "ind"),
        P("ind"),
        P(),
        P(),
        P(),
        P(("ind", "obs"), None),
        P(("ind", "obs"), None),
        P(None, "ind"),
    )
    return jax.shard_map(
        body,
        mesh=mesh,
        in_specs=placed,
        out_specs=(P(None, "obs"), P(("ind", "obs"), None), P(None, "ind")),
        check_vma=False,
    )
```

profile of v0, /device:TPU:1, one launch (start us, length us, event | category | flops | bytes accessed | tf_op | source)
XLA Modules:
  0.0 400.3 jit_solution(5778186779938577042)
XLA Ops:
  10.4 60.4 %while.1 = (s32[]{:T(128)}, f32[3,4224]{1,0:T(4,128)S(1)}, s32[32,2]{0,1:T(2,128)S(1)}, f32[32,3,128]{2,1,0:T(4,128)}, s32[]{:T(128)}) while((s32[]{:T(128)}, f32[3,4224]{1,0:T(4,128)S(1)}, s32[32,2]{0,1:T(2,128)S(1)}, f32[32,3,128]{2,1,0:T(4,128)}, s32[]{:T(128)}) %tuple.31), condition=%wide.while_cond, body=%wide.while_body.sunk | while | flops 2 | bytes 4197 | solution.py:55
  11.0 1.3 bitcast_dynamic-update-slice_fusion.2
  12.9 1.3 bitcast_dynamic-update-slice_fusion.2
  14.8 1.3 bitcast_dynamic-update-slice_fusion.2
  16.6 1.3 bitcast_dynamic-update-slice_fusion.2
  20.4 1.3 bitcast_dynamic-update-slice_fusion.2
  26.1 1.3 bitcast_dynamic-update-slice_fusion.2
  28.0 1.3 bitcast_dynamic-update-slice_fusion.2
  63.8 1.3 bitcast_dynamic-update-slice_fusion.2
  70.8 12.6 %all-to-all-start = ((f32[32,3,128]{2,1,0:T(4,128)}), f32[32,3,128]{2,1,0:T(4,128)S(1)}, u32[]{:S(2)}, u32[]{:S(2)}) async-start(f32[32,3,128]{2,1,0:T(4,128)} %get-tuple-element.10), calls=%async_computation | async-start | bytes 131072 | tf_op jit(solution)/shard_map/all_to_all | solution.py:58
  86.3 1.3 fusion.24
  87.6 5.6 %all-to-all-done = f32[32,3,128]{2,1,0:T(4,128)S(1)} async-done(((f32[32,3,128]{2,1,0:T(4,128)}), f32[32,3,128]{2,1,0:T(4,128)S(1)}, u32[]{:S(2)}, u32[]{:S(2)}) %all-to-all-start) | async-done | bytes 49184 | tf_op jit(solution)/shard_map/all_to_all | solution.py:58
  93.8 13.0 %gather_fusion = f32[2048,3]{1,0:T(8,128)S(1)} fusion(f32[32,3,128]{1,2,0:T(8,128)S(1)} %copy.17, s32[2048]{0:T(1024)S(1)} %bitcast.38), kind=kCustom, calls=%fused_computation | custom fusion | bytes 65536 | tf_op jit(solution)/shard_map/gather | solution.py:64
  109.3 10.1 %multiply_convert_fusion.1 = bf16[2048,1024]{1,0:T(8,128)(2,1)} fusion(f32[2048,6]{0,1:T(8,128)S(1)} %get-tuple-element.35, f32[]{:T(128)} %bitcast.10, f32[1024]{0:T(1024)S(1)} %bitcast.50, f32[2048]{0:T(1024)S(1)} %get-tuple-element.14, f32[]{:T(128)} %bitcast.8, f32[1024]{0:T(1024)S(1)} %bitcast.49, f32[2048]{0:T(1024)S(1)} %get-tuple-element.13, ...), kind=kOutput, calls=%fused_computation.6 | convolution fusion | flops 171972608 | bytes 4272136 | tf_op jit(solution)/shard_map/dot_general | solution.py:20
  119.4 7.5 %multiply_reduce_fusion = (f32[2048]{0:T(1024)S(1)}, bf16[2048,1024]{0,1:T(8,128)(2,1)S(1)}) fusion(bf16[2048,1024]{1,0:T(8,128)(2,1)} %multiply_convert_fusion.1, bf16[1024,1024]{1,0:T(8,128)(2,1)} %all-gather.3.cloned.1.call-done), kind=kOutput, calls=%fused_computation.4 | convolution fusion | flops 4301256704 | bytes 10493952 | tf_op jit(solution)/shard_map/dot_general | solution.py:80
  126.9 2.0 copy-done.1
  130.4 44.3 %all-gather.5.cloned.1.call-done = bf16[1024,1024]{1,0:T(8,128)(2,1)} async-done(((bf16[32,1024]{1,0:T(8,128)(2,1)}), bf16[1024,1024]{1,0:T(8,128)(2,1)}) %all-gather.5.cloned.1.call-update) | async-done | bytes 2097168 | tf_op jit(solution)/shard_map/all_gather | solution.py:78
  174.7 10.7 %multiply_reduce_fusion.1 = (f32[2048]{0:T(1024)S(1)}, f32[2048,1024]{0,1:T(8,128)}) fusion(bf16[2048,1024]{0,1:T(8,128)(2,1)} %copy-done.1, bf16[1024,1024]{1,0:T(8,128)(2,1)} %all-gather.5.cloned.1.call-done), kind=kOutput, calls=%fused_computation.5 | convolution fusion | flops 4299159552 | bytes 14688256 | tf_op jit(solution)/shard_map/dot_general | solution.py:82
  185.4 15.4 %psum.22 = f32[1,2048]{1,0:T(1,128)S(1)} all-reduce(f32[1,2048]{1,0:T(1,128)S(1)} %bitcast.45), channel_id=1, replica_groups=mesh['obs'=32,'ind'=8] {'ind'}, use_global_device_ids=true, to_apply=%region_8.9 | all-reduce | flops 2048 | bytes 16384 | tf_op jit(solution)/shard_map/psum | solution.py:89
  200.8 45.9 %all-reduce.4.cloned.1.call-done = f32[8,2048]{1,0:T(8,128)} async-done(((f32[8,2048]{1,0:T(8,128)}), f32[8,2048]{1,0:T(8,128)}) %all-reduce.4.cloned.1.call-update) | async-done | bytes 65552 | tf_op jit(solution)/shard_map/psum | solution.py:89
  248.7 10.7 %select_convert_fusion = bf16[1024,1024]{1,0:T(8,128)(2,1)} fusion(bf16[2048,1024]{0,1:T(8,128)(2,1)} %copy-done.1, f32[2048,1024]{0,1:T(8,128)} %get-tuple-element.37, f32[2048]{0:T(1024)S(1)} %broadcast_multiply_fusion.1), kind=kOutput, calls=%fused_computation.8 | convolution fusion | flops 4302307328 | bytes 14688256 | tf_op jit(solution)/shard_map/dot_general | solution.py:100
  259.6 3.4 fusion.12
  263.0 128.6 %psum.23 = f32[8,1024]{1,0:T(8,128)S(1)} all-reduce(f32[8,1024]{1,0:T(8,128)S(1)} %fusion.12), channel_id=1, replica_groups=mesh['obs'=32,'ind'=8] {'obs'}, use_global_device_ids=true, to_apply=%region_13.14 | all-reduce | flops 8192 | bytes 65536 | tf_op jit(solution)/shard_map/psum | solution.py:117
  392.2 1.6 fusion.7
  (142 shorter events, 63.3 us)
Async XLA Ops:
  7.2 77.5 %copy-start = (f32[6,6]{1,0:T(8,128)S(1)}, f32[6,6]{1,0:T(8,128)}, u32[]{:S(2)}) copy-start(f32[6,6]{1,0:T(8,128)} %param.16) | copy-start | bytes 436
  7.2 112.2 %all-gather.3.cloned.1.call-start = ((), (), s32[]{:S(2)}) async-start(), calls=%async_computation.2 | async-start | bytes 2162688 | tf_op jit(solution)/shard_map/all_gather | solution.py:77
  70.8 22.4 %all-to-all-start = ((f32[32,3,128]{2,1,0:T(4,128)}), f32[32,3,128]{2,1,0:T(4,128)S(1)}, u32[]{:S(2)}, u32[]{:S(2)}) async-start(f32[32,3,128]{2,1,0:T(4,128)} %get-tuple-element.10), calls=%async_computation | async-start | bytes 131072 | tf_op jit(solution)/shard_map/all_to_all | solution.py:58
  83.4 91.3 %all-gather.5.cloned.1.call-start = ((), (), s32[]{:S(2)}) async-start(), calls=%async_computation.4 | async-start | bytes 2162688 | tf_op jit(solution)/shard_map/all_gather | solution.py:78
  84.1 162.6 %all-reduce.4.cloned.1.call-start = ((), (), s32[]{:S(2)}) async-start(), calls=%async_computation.3 | async-start | bytes 131072 | tf_op jit(solution)/shard_map/psum | solution.py:89
  93.8 15.5 %copy-start.6 = (s32[1024]{0:T(1024)S(1)}, s32[1024]{0:T(1024)}, u32[]{:S(2)}) copy-start(s32[1024]{0:T(1024)} %param.15) | copy-start | bytes 12292
  119.4 9.5 %copy-start.4 = (bf16[8,1024]{1,0:T(8,128)(2,1)S(1)}, bf16[8,1024]{1,0:T(8,128)(2,1)}, u32[]{:S(2)}) copy-start(bf16[8,1024]{1,0:T(8,128)(2,1)} %param.21) | copy-start | bytes 49156
  126.9 2.0 copy-start.1
  130.2 117.5 %copy-start.5 = (f32[8]{0:T(128)S(1)}, f32[8]{0:T(128)}, u32[]{:S(2)}) copy-start(f32[8]{0:T(128)} %param.18) | copy-start | bytes 100
  130.2 262.0 %reduce-scatter.2.cloned.1.call-start = ((), (), s32[]{:S(2)}) async-start(), calls=%async_computation.5 | async-start | bytes 2162688 | tf_op jit(solution)/shard_map/reduce_scatter | solution.py:104
  248.6 10.9 %copy-start.3 = (f32[8,2048]{1,0:T(8,128)}, f32[8,2048]{1,0:T(8,128)S(1)}, u32[]{:S(2)}) copy-start(f32[8,2048]{1,0:T(8,128)S(1)} %get-tuple-element.24) | copy-start | bytes 196612
  248.7 10.7 %copy-start.2 = (bf16[32,1024]{1,0:T(8,128)(2,1)S(1)}, bf16[32,1024]{1,0:T(8,128)(2,1)}, u32[]{:S(2)}) copy-start(bf16[32,1024]{1,0:T(8,128)(2,1)} %param.20) | copy-start | bytes 196612
Sparse Core Ops, SparseCore 0:
  10.8 84.2 all-gather.2
  97.9 76.8 all-gather.4
  177.9 68.7 all-reduce.3
  259.5 119.2 reduce-scatter.1
where the time goes:
time: 405 us; the launch traced here: 400 us
  blocking collectives  144 us (36%)
  waiting for transfers between devices  97.2 us (24%)
  local copies, waits for them, and re-layouts  79.1 us (20%)
  matrix products  43.9 us (11%)
  between operations  14 us (3%)
  starting transfers between devices  12.9 us (3%)
  other arithmetic  9.17 us (2%)
    psum x1, blocking collectives, body(): lax.psum(mean_term, 'obs') - variational_mean.astype(jnp.float32)  129 us
    gather x96, local copies, waits for them, and re-layouts  60.3 us
    psum x1, waiting for transfers between devices, body(): mean_sum, var_sum = lax.psum((mean_part, var_part), 'ind')  45.9 us
    all_gather x1, waiting for transfers between devices, body(): lax.all_gather(variational_chol, 'obs', axis=0, tiled=True)  44.3 us
    psum x1, blocking collectives, body(): mean_sum, var_sum = lax.psum((mean_part, var_part), 'ind')  15.4 us
    gather x1, local copies, waits for them, and re-layouts, body(): arrived = incoming[source, :, position - begin_row].T  13 us
    all_to_all x1, starting transfers between devices, body(): lax.all_to_all(outgoing, 'obs', split_axis=0, concat_axis=0, tiled=True)  12.6 us
    dot_general x1, matrix products, body(): jnp.dot(whitened_bf, chol_block, preferred_element_type=jnp.float32)  10.7 us
  transfers between devices with their start and end apart: 5, of which 3 were waited for; matrix products, arithmetic and copies ran while one was open for 29% of the time, Pallas kernels for 0%

commit v1 on v0

v1 whole, which is shorter than its diff:
```python
import functools
import math

import jax
import jax.numpy as jnp
from jax import lax
from jax.experimental import pallas as pl
from jax.experimental.pallas import tpu as pltpu
from jax.sharding import PartitionSpec as P

C = 8
NB = 6
ROWS = 2048
MB = 1024
MESH = pl.DeviceIdType.MESH
F32 = jnp.float32
BF16 = jnp.bfloat16
ROOT = math.sqrt(0.5 * math.log2(math.e))


def dot_nn(a, b):
    return jnp.dot(a, b, preferred_element_type=F32)


def dot_nt(a, b):
    return lax.dot_general(a, b, (((1,), (1,)), ((), ())), preferred_element_type=F32)


def exact_pick(hot, rows):
    return jnp.dot(hot, rows, precision=lax.Precision.HIGHEST, preferred_element_type=F32)


def kernel(
    coords_ref, codes_ref, plan_ref, centers_ref, bands_ref, mix_ref, ls_ref, scales_ref,
    w_in, l_in, m_in,
    probs_out, gchol_out, gmean_out,
    held, sendbuf, incoming, feat, crow, tab, centers_s, mpad,
    wbuf, lbuf, kbuf, abuf, atbuf, bbuf, hbuf, sq,
    stats, gathered, pieces, ms,
    gbuf, r1, s1, r2, s2, r3,
    mt0, mt1, mt2, rm1, rm2, rm3,
    route_s, route_r, agw_s, agw_r, agl_s, agl_r,
    st_s, st_r, pr_s, pr_r, p1_s, p1_r, p2_s, p2_r, p3_s, p3_r,
    m12_s, m12_r, m3_s, m3_r,
):
    me = lax.axis_index("obs")
    ib = lax.axis_index("ind")
    z = me // 4
    xh = (me // 2) % 2
    c = me % 2
    oxh = 1 - xh
    oc = 1 - c
    zp = (z + 1) % 8
    zm = (z + 7) % 8

    def at(zz, xx, cc):
        return (zz * 4 + xx * 2 + cc, ib)

    def remote(src, dst, ssem, rsem, dev):
        return pltpu.make_async_remote_copy(
            src_ref=src, dst_ref=dst, send_sem=ssem, recv_sem=rsem, device_id=dev, device_id_type=MESH
        )

    r3[...] = jnp.zeros_like(r3)

    barrier = pltpu.get_barrier_semaphore()

    def greet_obs(d, carry):
        pl.semaphore_signal(barrier, inc=1, device_id=((me + d) % 32, ib), device_id_type=MESH)
        return carry

    def greet_ind(d, carry):
        pl.semaphore_signal(barrier, inc=1, device_id=(me, (ib + d) % 8), device_id_type=MESH)
        return carry

    lax.fori_loop(1, 32, greet_obs, 0)
    lax.fori_loop(1, 8, greet_ind, 0)

    for b in range(32):
        held[0, b : b + 1, :] = coords_ref[0:1, b * 128 : b * 128 + 128]
        held[1, b : b + 1, :] = coords_ref[1:2, b * 128 : b * 128 + 128]
    plan = plan_ref[...]
    sub = lax.broadcasted_iota(jnp.int32, (32, 32), 0)
    lan = lax.broadcasted_iota(jnp.int32, (32, 32), 1)
    plan_row = jnp.sum(jnp.where(sub == me, plan, 0), axis=0, keepdims=True)
    start = jnp.sum(jnp.where(lan < sub, plan_row, 0), axis=1, keepdims=True)
    choose = (lan == start).astype(F32)
    sendbuf[:, 0, :] = exact_pick(choose, held[0])
    sendbuf[:, 1, :] = exact_pick(choose, held[1])
    sendbuf[:, 2, :] = exact_pick(choose, codes_ref[...].astype(F32))
    sendbuf[:, 3, :] = jnp.zeros((32, 128), F32)
    incoming[me] = sendbuf[me]
    wbuf[z, xh, c] = w_in[...]
    lbuf[z, xh, c] = l_in[...]

    pl.semaphore_wait(barrier, 38)

    def route_copy(d):
        peer = (me + d) % 32
        return remote(sendbuf.at[peer], incoming.at[me], route_s.at[d], route_r.at[d], (peer, ib))

    def route_start(d, carry):
        route_copy(d).start()
        return carry

    lax.fori_loop(1, 32, route_start, 0)

    class Gather:
        def __init__(self, own, buf, ss, rs):
            self.own, self.buf, self.ss, self.rs = own, buf, ss, rs

        def x_copy(self):
            b = self.buf
            return remote(self.own, b.at[z, xh, c], self.ss.at[0], self.rs.at[0], at(z, oxh, c))

        def x_recv(self):
            b = self.buf
            return remote(self.own, b.at[z, oxh, c], self.ss.at[0], self.rs.at[0], at(z, oxh, c))

        def unit(self, zz, idx, dev):
            b = self.buf
            return remote(b.at[zz, :, c], b.at[zz, :, c], self.ss.at[idx], self.rs.at[idx], dev)

        def half(self, zz, j, idx, dev):
            b = self.buf
            return remote(b.at[zz, j, c], b.at[zz, j, c], self.ss.at[idx], self.rs.at[idx], dev)

        def up(self, k):
            if k < 4:
                return self.unit((z + 8 - (k - 1)) % 8, k, at(zp, xh, c))
            return self.half((z + 5) % 8, 0, 4, at(zp, xh, c))

        def down(self, k):
            if k < 4:
                return self.unit((z + (k - 1)) % 8, 4 + k, at(zm, xh, c))
            return self.half((z + 3) % 8, 1, 8, at(zm, xh, c))

        def up_recv(self, k):
            if k < 4:
                return self.unit((z + 8 - k) % 8, k, at(zp, xh, c))
            return self.half((z + 4) % 8, 0, 4, at(zp, xh, c))

        def down_recv(self, k):
            if k < 4:
                return self.unit((z + k) % 8, 4 + k, at(zm, xh, c))
            return self.half((z + 4) % 8, 1, 8, at(zm, xh, c))

        def core(self, q):
            zz = self.core_unit(q)
            return self.unit(zz, 9 + q, at(z, xh, oc))

        def core_recv(self, q):
            b = self.buf
            zz = self.core_unit(q)
            return remote(b.at[zz, :, oc], b.at[zz, :, oc], self.ss.at[9 + q], self.rs.at[9 + q], at(z, xh, oc))

        def core_unit(self, q):
            if q == 0:
                return z
            if q == 7:
                return (z + 4) % 8
            k = (q + 1) // 2
            return (z + 8 - k) % 8 if q % 2 == 1 else (z + k) % 8

        def begin(self):
            self.x_copy().start()

        def step(self, k):
            if k == 0:
                self.x_recv().wait_recv()
                self.up(1).start()
                self.down(1).start()
                self.core(0).start()
                return
            self.up_recv(k).wait_recv()
            self.down_recv(k).wait_recv()
            if k < 4:
                self.up(k + 1).start()
                self.down(k + 1).start()
                self.core(2 * k - 1).start()
                self.core(2 * k).start()
            else:
                self.core(7).start()

        def end(self):
            for q in range(8):
                self.core_recv(q).wait_recv()

        def drain(self):
            self.x_copy().wait_send()
            for k in range(1, 5):
                self.up(k).wait_send()
                self.down(k).wait_send()
            for q in range(8):
                self.core(q).wait_send()

    gw = Gather(w_in, wbuf, agw_s, agw_r)
    gl = Gather(l_in, lbuf, agl_s, agl_r)
    gw.begin()
    gl.begin()

    ls0 = jnp.full((1, MB), ls_ref[0], F32)
    ls1 = jnp.full((1, MB), ls_ref[1], F32)
    centers_s[0:1, :] = centers_ref[0:1, :] * (ROOT / ls0)
    centers_s[1:2, :] = centers_ref[1:2, :] * (ROOT / ls1)
    kinds8 = lax.broadcasted_iota(jnp.int32, (8, 128), 0)
    for s in range(8):
        band = jnp.broadcast_to(bands_ref[s : s + 1, :], (8, 128))
        total = (band == kinds8).astype(F32)
        for i in range(NB):
            picked = jnp.zeros((8, 128), F32)
            column = jnp.zeros((8, 128), F32)
            for k in range(NB):
                picked = jnp.where(band == k, mix_ref[k, i], picked)
                column = jnp.where(kinds8 == k, mix_ref[k, i], column)
            total = total + column * picked
        high = total.astype(BF16).astype(F32)
        rest = total - high
        middle = rest.astype(BF16).astype(F32)
        low = rest - middle
        zeros = jnp.zeros((104, 128), F32)
        tab[:, s * 128 : (s + 1) * 128] = jnp.concatenate([high, middle, low, zeros], axis=0).astype(BF16)
    mpad[...] = jnp.concatenate([m_in[...].astype(F32), jnp.zeros((120, MB), F32)], axis=0).astype(BF16)

    plan_col = jnp.sum(jnp.where(lan == me, plan, 0), axis=1, keepdims=True)
    before = jnp.sum(jnp.where(sub < lan, plan_col, 0), axis=0, keepdims=True)
    sub16 = lax.broadcasted_iota(jnp.int32, (16, 32), 0)
    lan16 = lax.broadcasted_iota(jnp.int32, (16, 32), 1)
    source = jnp.sum((before <= sub16).astype(jnp.int32), axis=1, keepdims=True) - 1
    source_hot = (lan16 == source).astype(F32)

    gw.step(0)

    def route_wait(d, carry):
        src = (me + 32 - d) % 32
        remote(sendbuf.at[src], incoming.at[src], route_s.at[d], route_r.at[d], (src, ib)).wait_recv()
        return carry

    lax.fori_loop(1, 32, route_wait, 0)

    st = ROOT / jnp.full((1, 128), ls_ref[0], F32)
    sw = ROOT / jnp.full((1, 128), ls_ref[1], F32)
    code = exact_pick(source_hot, incoming[:, 2, :])
    label = jnp.zeros((16, 128), F32)
    for n in range(1, C):
        label = label + (code >= float(NB * n)).astype(F32)
    band = code - float(NB) * label
    feat[:, 0, :] = exact_pick(source_hot, incoming[:, 0, :]) * st
    feat[:, 1, :] = exact_pick(source_hot, incoming[:, 1, :]) * sw
    feat[:, 2, :] = band
    for k in range(3, 8):
        feat[:, k, :] = jnp.zeros((16, 128), F32)
    for k in range(16):
        lanes = slice((k % 2) * 128, (k % 2) * 128 + 128)
        crow[k // 2, 0:1, lanes] = label[k : k + 1, :]
        crow[k // 2, 1:2, lanes] = band[k : k + 1, :]

    lane = lax.broadcasted_iota(jnp.int32, (128, 128), 1)
    kind = (lane % 8).astype(F32)
    live = lane < 24

    def cov_block(b, carry):
        cols = jnp.transpose(feat[b])
        t = cols[:, 0:1]
        w = cols[:, 1:2]
        hot = jnp.where(live & (cols[:, 2:3] == kind), 1.0, 0.0).astype(BF16)
        rows = pl.ds(pl.multiple_of(b * 128, 128), 128)
        for s in range(4):
            lanes = slice(s * 256, s * 256 + 256)
            dt = t - centers_s[0:1, lanes]
            dw = w - centers_s[1:2, lanes]
            mixing = dot_nn(hot, tab[:, lanes])
            kbuf[rows, lanes] = (jnp.exp2(-(dt * dt + dw * dw)) * mixing).astype(BF16)
        return carry

    for part in range(4):
        lax.fori_loop(4 * part, 4 * part + 4, cov_block, 0)
        gw.step(part + 1)
    gl.step(0)
    gw.end()

    for part in range(4):
        rows = slice(part * 512, part * 512 + 512)
        for n in range(4):
            lanes = slice(n * 256, n * 256 + 256)
            a = dot_nn(kbuf[rows, :], wbuf[:, :, :, :, lanes].reshape(MB, 256))
            abuf[rows, lanes] = a.astype(BF16)
            squares = a[:, :128] * a[:, :128] + a[:, 128:] * a[:, 128:]
            if n == 0:
                sq[rows, :] = squares
            else:
                sq[rows, :] += squares
        gl.step(part + 1)
    gl.end()

    lane256 = lax.broadcasted_iota(jnp.int32, (256, 128), 1)

    def stat_copy(i):
        return remote(stats.at[i], gathered.at[ib], st_s.at[i], st_r.at[ib], (me, i))

    def b_block(i, carry):
        rows = pl.ds(pl.multiple_of(i * 256, 256), 256)
        squares = -sq[rows, :]
        for n in range(4):
            lanes = slice(n * 256, n * 256 + 256)
            deep = slice(n * 256, MB)
            lower = lbuf[2 * n :, :, :, :, lanes].reshape(MB - n * 256, 256)
            b = dot_nn(abuf[rows, deep], lower)
            bbuf[rows, lanes] = b
            squares = squares + (b[:, :128] * b[:, :128] + b[:, 128:] * b[:, 128:])
        means = dot_nt(abuf[rows, :], mpad[...])
        var = jnp.sum(squares, axis=1, keepdims=True)
        both = jnp.transpose(jnp.where(lane256 == 8, var, means))
        stats[i] = both[0:16, :]

        @pl.when(i != ib)
        def _():
            stat_copy(i).start()

        @pl.when(i == ib)
        def _():
            gathered[ib] = both[0:16, :]

        return carry

    lax.fori_loop(0, 8, b_block, 0)

    def flip(i, carry):
        rows = pl.ds(pl.multiple_of(i * 256, 256), 256)
        atbuf[:, rows] = jnp.transpose(abuf[rows, :])
        return carry

    lax.fori_loop(0, 3, flip, 0)

    def stat_wait(d, carry):
        src = (ib + d) % 8
        remote(stats.at[src], gathered.at[src], st_s.at[src], st_r.at[src], (me, src)).wait_recv()
        return carry

    lax.fori_loop(1, 8, stat_wait, 0)

    scale = jnp.zeros((8, 256), F32)
    class_ids = lax.broadcasted_iota(jnp.int32, (8, 256), 0)
    for n in range(C):
        scale = jnp.where(class_ids == n, scales_ref[n], scale)

    both = gathered[0]
    for p in range(1, 8):
        both = both + gathered[p]
    band = crow[ib, 1:2, :]
    own = jnp.zeros((1, 256), F32)
    for k in range(NB):
        value = jnp.float32(1.0)
        for i in range(NB):
            value = value + mix_ref[k, i] * mix_ref[k, i]
        own = jnp.where(band == float(k), value, own)
    logits = both[0:8, :] + 0.5 * scale * (both[8:9, :] + own)
    weights = jnp.exp(logits)
    chances = weights / jnp.sum(weights, axis=0, keepdims=True)
    pieces[ib] = chances

    def piece_copy(d):
        dev = (ib + d) % 8
        return remote(pieces.at[ib], pieces.at[ib], pr_s.at[d], pr_r.at[d], (me, dev))

    def piece_start(d, carry):
        piece_copy(d).start()
        return carry

    lax.fori_loop(1, 8, piece_start, 0)
    lax.fori_loop(3, 8, flip, 0)

    def piece_wait(d, carry):
        src = (ib + 8 - d) % 8
        remote(pieces.at[src], pieces.at[src], pr_s.at[d], pr_r.at[d], (me, src)).wait_recv()
        return carry

    lax.fori_loop(1, 8, piece_wait, 0)

    classes = class_ids.astype(F32)
    for p in range(8):
        lanes = slice(p * 256, p * 256 + 256)
        ch = pieces[p]
        probs_out[:, lanes] = ch
        slope = jnp.where(crow[p, 0:1, :] == classes, 1.0, 0.0) - ch
        ms[:, lanes] = jnp.concatenate([slope, jnp.zeros((8, 256), F32)], axis=0).astype(BF16)

    mt0[...] = dot_nn(ms[...], abuf[...])[0:8, :]
    mean1 = remote(mt0, rm1, m12_s.at[0], m12_r.at[0], at(z, xh, oc))
    mean1.start()

    def h_block(i, carry):
        rows = pl.ds(pl.multiple_of(i * 256, 256), 256)
        slope = -jnp.sum(pieces[i] * scale, axis=0, keepdims=True)
        column = jnp.transpose(jnp.broadcast_to(slope, (8, 256)))[:, 0:1]
        hbuf[rows, :] = (column * bbuf[rows, :]).astype(BF16)
        return carry

    lax.fori_loop(0, 8, h_block, 0)

    def m3_copy(d):
        return remote(mt2, rm3.at[z], m3_s.at[d], m3_r.at[d], at((z + d) % 8, xh, c))

    mean2 = remote(mt1, rm2, m12_s.at[1], m12_r.at[1], at(z, oxh, c))

    def p1_copy(n):
        lanes = pl.ds(n * 256, 256)
        return remote(
            gbuf.at[pl.ds(2 * n, 8 - 2 * n), :, oc, :, lanes],
            r1.at[pl.ds(2 * n, 8 - 2 * n), :, :, lanes],
            p1_s.at[n], p1_r.at[n], at(z, xh, oc),
        )

    def p2_copy(n):
        lanes = pl.ds(n * 256, 256)
        return remote(
            s1.at[pl.ds(2 * n, 8 - 2 * n), oxh, :, lanes],
            r2.at[pl.ds(2 * n, 8 - 2 * n), :, lanes],
            p2_s.at[n], p2_r.at[n], at(z, oxh, c),
        )

    def p3_copy(n, zz):
        lanes = pl.ds(n * 256, 256)
        return remote(
            s2.at[zz, :, lanes], r3.at[z, :, lanes], p3_s.at[n, zz], p3_r.at[n, z], at(zz, xh, c)
        )

    def stage1(n):
        lanes = slice(n * 256, n * 256 + 256)
        g = dot_nn(atbuf[n * 256 :, :], hbuf[:, lanes]).astype(BF16)
        gbuf[2 * n :, :, :, :, lanes] = g.reshape(8 - 2 * n, 2, 2, 32, 256)
        p1_copy(n).start()

    def stage2(n):
        p1_copy(n).wait_recv()
        lanes = pl.ds(n * 256, 256)

        def add(zz, carry):
            for j in range(2):
                total = gbuf[zz, j, c, :, lanes].astype(F32) + r1[zz, j, :, lanes].astype(F32)
                s1[zz, j, :, lanes] = total.astype(BF16)
            return carry

        lax.fori_loop(2 * n, 8, add, 0)
        p2_copy(n).start()

    def stage3(n):
        p2_copy(n).wait_recv()
        lanes = pl.ds(n * 256, 256)

        def add(zz, carry):
            total = s1[zz, xh, :, lanes].astype(F32) + r2[zz, :, lanes].astype(F32)
            s2[zz, :, lanes] = total.astype(BF16)

            @pl.when(zz != z)
            def _():
                p3_copy(n, zz).start()

            @pl.when(zz == z)
            def _():
                r3[z, :, lanes] = total.astype(BF16)

            return carry

        lax.fori_loop(2 * n, 8, add, 0)

    stage1(0)
    mean1.wait_recv()
    mt1[...] = mt0[...] + rm1[...]
    mean2.start()
    stage1(1)
    stage2(0)
    mean2.wait_recv()
    mt2[...] = mt1[...] + rm2[...]
    rm3[z] = mt2[...]

    def m3_start(d, carry):
        m3_copy(d).start()
        return carry

    lax.fori_loop(1, 8, m3_start, 0)
    stage1(2)
    stage2(1)
    stage3(0)
    stage1(3)
    stage2(2)
    stage3(1)
    stage2(3)
    stage3(2)
    stage3(3)

    def m3_wait(d, carry):
        src = (z + 8 - d) % 8
        remote(mt2, rm3.at[src], m3_s.at[d], m3_r.at[d], at(src, xh, c)).wait_recv()
        return carry

    lax.fori_loop(1, 8, m3_wait, 0)
    grad = rm3[0]
    for p in range(1, 8):
        grad = grad + rm3[p]
    gmean_out[...] = grad - m_in[...].astype(F32)

    def p3_wait(n):
        lanes = pl.ds(n * 256, 256)

        def one(d, carry):
            src = (z + 8 - d) % 8
            remote(
                s2.at[src, :, lanes], r3.at[src, :, lanes], p3_s.at[n, src], p3_r.at[n, src], at(src, xh, c)
            ).wait_recv()
            return carry

        @pl.when(z >= 2 * n)
        def _():
            lax.fori_loop(1, 8, one, 0)

    for n in range(4):
        p3_wait(n)
    data = r3[0].astype(F32)
    for p in range(1, 8):
        data = data + r3[p].astype(F32)
    column_ids = lax.broadcasted_iota(jnp.int32, (32, MB), 1)
    row_ids = lax.broadcasted_iota(jnp.int32, (32, MB), 0) + me * 32
    own_chol = l_in[...].astype(F32)
    on_diag = column_ids == row_ids
    diagonal = jnp.sum(jnp.where(on_diag, own_chol, 0.0), axis=1, keepdims=True)
    gchol_out[...] = (
        jnp.where(column_ids <= row_ids, data, 0.0) - own_chol + jnp.where(on_diag, 1.0 / diagonal, 0.0)
    )

    def route_drain(d, carry):
        route_copy(d).wait_send()
        return carry

    lax.fori_loop(1, 32, route_drain, 0)
    gw.drain()
    gl.drain()

    def ind_drain(d, carry):
        stat_copy((ib + d) % 8).wait_send()
        piece_copy(d).wait_send()
        m3_copy(d).wait_send()
        return carry

    lax.fori_loop(1, 8, ind_drain, 0)
    mean1.wait_send()
    mean2.wait_send()
    for n in range(4):
        p1_copy(n).wait_send()
        p2_copy(n).wait_send()

        def p3_drain(zz, carry):
            @pl.when(zz != z)
            def _():
                p3_copy(n, zz).wait_send()

            return carry

        lax.fori_loop(2 * n, 8, p3_drain, 0)


def body(
    obs_coords, obs_codes, route_plan, inducing_coords, inducing_bands, band_mix, lengthscales,
    class_scales, prior_factor, variational_chol, variational_mean,
):
    vmem = pl.BlockSpec(memory_space=pltpu.VMEM)
    smem = pl.BlockSpec(memory_space=pltpu.SMEM)
    dma = pltpu.SemaphoreType.DMA
    return pl.pallas_call(
        kernel,
        out_shape=(
            jax.ShapeDtypeStruct((C, ROWS), F32),
            jax.ShapeDtypeStruct((32, MB), F32),
            jax.ShapeDtypeStruct((C, MB), F32),
        ),
        in_specs=[vmem, vmem, vmem, vmem, vmem, smem, smem, smem, vmem, vmem, vmem],
        out_specs=(vmem, vmem, vmem),
        scratch_shapes=[
            pltpu.VMEM((2, 32, 128), F32),
            pltpu.VMEM((32, 4, 128), F32),
            pltpu.VMEM((32, 4, 128), F32),
            pltpu.VMEM((16, 8, 128), F32),
            pltpu.VMEM((8, 2, 256), F32),
            pltpu.VMEM((128, MB), BF16),
            pltpu.VMEM((2, MB), F32),
            pltpu.VMEM((128, MB), BF16),
            pltpu.VMEM((8, 2, 2, 32, MB), BF16),
            pltpu.VMEM((8, 2, 2, 32, MB), BF16),
            pltpu.VMEM((ROWS, MB), BF16),
            pltpu.VMEM((ROWS, MB), BF16),
            pltpu.VMEM((MB, ROWS), BF16),
            pltpu.VMEM((ROWS, MB), F32),
            pltpu.VMEM((ROWS, MB), BF16),
            pltpu.VMEM((ROWS, 128), F32),
            pltpu.VMEM((8, 16, 256), F32),
            pltpu.VMEM((8, 16, 256), F32),
            pltpu.VMEM((8, 8, 256), F32),
            pltpu.VMEM((16, ROWS), BF16),
            pltpu.VMEM((8, 2, 2, 32, MB), BF16),
            pltpu.VMEM((8, 2, 32, MB), BF16),
            pltpu.VMEM((8, 2, 32, MB), BF16),
            pltpu.VMEM((8, 32, MB), BF16),
            pltpu.VMEM((8, 32, MB), BF16),
            pltpu.VMEM((8, 32, MB), BF16),
            pltpu.VMEM((8, MB), F32),
            pltpu.VMEM((8, MB), F32),
            pltpu.VMEM((8, MB), F32),
            pltpu.VMEM((8, MB), F32),
            pltpu.VMEM((8, MB), F32),
            pltpu.VMEM((8, 8, MB), F32),
            dma((32,)), dma((32,)), dma((17,)), dma((17,)), dma((17,)), dma((17,)),
            dma((8,)), dma((8,)), dma((8,)), dma((8,)),
            dma((4,)), dma((4,)), dma((4,)), dma((4,)), dma((4, 8)), dma((4, 8)),
            dma((2,)), dma((2,)), dma((8,)), dma((8,)),
        ],
        compiler_params=pltpu.CompilerParams(
            collective_id=0, has_side_effects=True, vmem_limit_bytes=60 << 20
        ),
        name="elbo_step",
    )(
        obs_coords, obs_codes.reshape(32, 128), route_plan, inducing_coords,
        inducing_bands.reshape(8, 128), band_mix, lengthscales, class_scales,
        prior_factor, variational_chol, variational_mean,
    )


def solution(mesh):
    placed = (
        P(None, "obs"), P("obs"), P(), P(None, "ind"), P("ind"), P(), P(), P(),
        P(("ind", "obs"), None), P(("ind", "obs"), None), P(None, "ind"),
    )
    return jax.shard_map(
        body,
        mesh=mesh,
        in_specs=placed,
        out_specs=(P(None, "obs"), P(("ind", "obs"), None), P(None, "ind")),
        check_vma=False,
    )
```

time: 405 us -> 99.2 us (0.24); the launches traced: 400 us -> 99 us
  blocking collectives: 144 us -> 0 us
  waiting for transfers between devices: 97.2 us -> 0 us
  Pallas kernels: 0 us -> 95.5 us
  local copies, waits for them, and re-layouts: 79.1 us -> 2.88 us
  matrix products: 43.9 us -> 0 us
  between operations: 14 us -> 0.65 us
  starting transfers between devices: 12.9 us -> 0 us
  other arithmetic: 9.17 us -> 0 us
    psum x2 -> x0, blocking collectives: 144 us -> none  [the longest x1 129 us: body(): lax.psum(mean_term, 'obs') - variational_mean.astype(jnp.float32)]
    pallas_call x0 -> x1, Pallas kernels: none -> 95.5 us  [body(): pl.pallas_call(kernel, out_shape=(jax.ShapeDtypeStruct((C, ROWS), F32), j...]
    gather x97 -> x0, local copies, waits for them, and re-layouts: 73.4 us -> none
    psum x1 -> x0, waiting for transfers between devices: 45.9 us -> none  [body(): mean_sum, var_sum = lax.psum((mean_part, var_part), 'ind')]
    all_gather x2 -> x0, waiting for transfers between devices: 44.3 us -> none  [the longest x1 44.3 us: body(): lax.all_gather(variational_chol, 'obs', axis=0, tiled=True)]
    dot_general x8 -> x0, matrix products: 43.9 us -> none  [the longest x1 10.7 us: body(): jnp.dot(whitened_bf, chol_block, preferred_element_type=jnp.float32)]
    all_to_all x1 -> x0, starting transfers between devices: 12.6 us -> none  [body(): lax.all_to_all(outgoing, 'obs', split_axis=0, concat_axis=0, tiled=True)]
    all_to_all x1 -> x0, waiting for transfers between devices: 5.56 us -> none  [body(): lax.all_to_all(outgoing, 'obs', split_axis=0, concat_axis=0, tiled=True)]
  transfers between devices with their start and end apart: 5 -> 0, of which waited for: 3 -> 0; matrix products, arithmetic and copies ran while one was open for 29% -> 0% of each run, Pallas kernels for 0% -> 0%
where the time goes in v1:
time: 99.2 us; the launch traced here: 99 us
  Pallas kernels  95.5 us (96%)
  local copies, waits for them, and re-layouts  2.88 us (3%)
    pallas_call x1, Pallas kernels, body(): pl.pallas_call(kernel, out_shape=(jax.ShapeDtypeStruct((C, ROWS), F32), j...  95.5 us
    unnamed x7, local copies, waits for them, and re-layouts  2.88 us

profile of v1, /device:TPU:1, one launch (start us, length us, event | category | flops | bytes accessed | tf_op | source)
XLA Modules:
  0.0 99.0 jit_solution(191267612417261086)
XLA Ops:
  0.6 95.5 %elbo_step.1 = (f32[8,2048]{1,0:T(8,128)}, f32[32,1024]{1,0:T(8,128)}, f32[8,1024]{1,0:T(8,128)}) custom-call(f32[2,4096]{1,0:T(2,128)} %coords_ref.1, s32[32,128]{1,0:T(8,128)} %bitcast.2, s32[32,32]{1,0:T(8,128)} %plan_ref.1, f32[2,1024]{1,0:T(2,128)} %centers_ref.1, s32[8,128]{1,0:T(8,128)} %bitcast.3, f32[6,6]{1,0:T(8,128)} %mix_ref.1, f32[2]{0:T(128)} %ls_ref.1, ...), custom_call_target="tpu_custom_call" | custom-call | tf_op jit(solution)/shard_map/elbo_step/pallas_call | solution.py:569
  96.1 0.0 copy-start
  96.1 1.5 %copy.17 = f32[8,2048]{1,0:T(8,128)} copy(f32[8,2048]{1,0:T(8,128)} %get-tuple-element.6) | data formatting | bytes 131072
  97.6 0.0 copy-done
  97.7 0.0 copy-start.1
  97.7 0.7 copy.18
  98.3 0.1 copy-done.1
  98.4 0.6 copy.19
Async XLA Ops:
  96.1 1.5 %copy-start = (f32[32,1024]{1,0:T(8,128)S(1)}, f32[32,1024]{1,0:T(8,128)}, u32[]{:S(2)}) copy-start(f32[32,1024]{1,0:T(8,128)} %get-tuple-element.7) | copy-start | bytes 393220
  97.7 0.8 copy-start.1

commit v2 on v1

--- a/solution.py
+++ b/solution.py
@@ -36,12 +36,12 @@
     probs_out, gchol_out, gmean_out,
     held, sendbuf, incoming, feat, crow, tab, centers_s, mpad,
     wbuf, lbuf, kbuf, abuf, atbuf, bbuf, hbuf, sq,
-    stats, gathered, pieces, ms,
+    terms, ms,
     gbuf, r1, s1, r2, s2, r3,
-    mt0, mt1, mt2, rm1, rm2, rm3,
+    mt0, mt1, mt2, rm1, rm2, rm3, quarters,
     route_s, route_r, agw_s, agw_r, agl_s, agl_r,
-    st_s, st_r, pr_s, pr_r, p1_s, p1_r, p2_s, p2_r, p3_s, p3_r,
-    m12_s, m12_r, m3_s, m3_r,
+    st_s, st_r, p1_s, p1_r, p2_s, p2_r, p3_s, p3_r,
+    m12_s, m12_r, m3_s, m3_r, m4_s, m4_r,
 ):
     me = lax.axis_index("obs")
     ib = lax.axis_index("ind")
@@ -106,98 +106,107 @@
     lax.fori_loop(1, 32, route_start, 0)
 
     class Gather:
-        def __init__(self, own, buf, ss, rs):
-            self.own, self.buf, self.ss, self.rs = own, buf, ss, rs
-
-        def x_copy(self):
-            b = self.buf
-            return remote(self.own, b.at[z, xh, c], self.ss.at[0], self.rs.at[0], at(z, oxh, c))
-
-        def x_recv(self):
-            b = self.buf
-            return remote(self.own, b.at[z, oxh, c], self.ss.at[0], self.rs.at[0], at(z, oxh, c))
-
-        def unit(self, zz, idx, dev):
-            b = self.buf
-            return remote(b.at[zz, :, c], b.at[zz, :, c], self.ss.at[idx], self.rs.at[idx], dev)
-
-        def half(self, zz, j, idx, dev):
-            b = self.buf
-            return remote(b.at[zz, j, c], b.at[zz, j, c], self.ss.at[idx], self.rs.at[idx], dev)
-
-        def up(self, k):
-            if k < 4:
-                return self.unit((z + 8 - (k - 1)) % 8, k, at(zp, xh, c))
-            return self.half((z + 5) % 8, 0, 4, at(zp, xh, c))
-
-        def down(self, k):
-            if k < 4:
-                return self.unit((z + (k - 1)) % 8, 4 + k, at(zm, xh, c))
-            return self.half((z + 3) % 8, 1, 8, at(zm, xh, c))
-
-        def up_recv(self, k):
-            if k < 4:
-                return self.unit((z + 8 - k) % 8, k, at(zp, xh, c))
-            return self.half((z + 4) % 8, 0, 4, at(zp, xh, c))
-
-        def down_recv(self, k):
-            if k < 4:
-                return self.unit((z + k) % 8, 4 + k, at(zm, xh, c))
-            return self.half((z + 4) % 8, 1, 8, at(zm, xh, c))
-
-        def core(self, q):
-            zz = self.core_unit(q)
-            return self.unit(zz, 9 + q, at(z, xh, oc))
-
-        def core_recv(self, q):
-            b = self.buf
-            zz = self.core_unit(q)
-            return remote(b.at[zz, :, oc], b.at[zz, :, oc], self.ss.at[9 + q], self.rs.at[9 + q], at(z, xh, oc))
-
-        def core_unit(self, q):
-            if q == 0:
-                return z
-            if q == 7:
-                return (z + 4) % 8
-            k = (q + 1) // 2
-            return (z + 8 - k) % 8 if q % 2 == 1 else (z + k) % 8
+        def __init__(self, own, buf, ss, rs, triangular):
+            self.own, self.buf, self.ss, self.rs, self.triangular = own, buf, ss, rs, triangular
+
+        def widths(self, zz, fn):
+            if not self.triangular:
+                fn(slice(None))
+                return
+            for v in range(4):
+
+                @pl.when(zz // 2 == v)
+                def _():
+                    fn(pl.ds(0, (v + 1) * 256))
+
+        def shard(self, zz, j, cc, lanes):
+            if self.triangular:
+                return self.buf.at[zz, j, cc, :, lanes]
+            return self.buf.at[zz, j, cc]
+
+        def go(self, op, zz, j, cc, idx, dev, mine=False):
+            def fn(lanes):
+                dst = self.shard(zz, j, cc, lanes)
+                src = dst
+                if mine:
+                    src = self.own.at[:, lanes] if self.triangular else self.own
+                copy = remote(src, dst, self.ss.at[idx], self.rs.at[idx], dev)
+                getattr(copy, op)()
+
+            self.widths(zz, fn)
+
+        def half(self, stream):
+            return xh if stream == 0 else oxh
+
+        def up(self, op, stream, k):
+            zz = (z + 8 - (k - 1)) % 8
+            self.go(op, zz, self.half(stream), c, 7 * stream + k, at(zp, xh, c), stream == 0 and k == 1)
+
+        def down(self, op, stream, k):
+            zz = (z + k - 1) % 8
+            self.go(op, zz, self.half(stream), c, 7 * stream + 3 + k, at(zm, xh, c), stream == 0 and k == 1)
+
+        def fourth(self, op, stream):
+            j = self.half(stream)
+            self.go(op, (z + 5 + 6 * j) % 8, j, c, 7 * stream + 7, at((z + 1 + 6 * j) % 8, xh, c))
+
+        def unit(self, q):
+            return (z + (0, 7, 6, 5, 1, 2, 3, 4)[q]) % 8
+
+        def core(self, op, stream, q):
+            mine = stream == 0 and q == 0
+            self.go(op, self.unit(q), self.half(stream), c, 15 + 8 * stream + q, at(z, xh, oc), mine)
+
+        def x_copy(self, op):
+            self.go(op, z, xh, c, 0, at(z, oxh, c), True)
 
         def begin(self):
-            self.x_copy().start()
-
-        def step(self, k):
+            self.up("start", 0, 1)
+            self.down("start", 0, 1)
+            self.x_copy("start")
+            self.core("start", 0, 0)
+
+        def step(self, stream, k):
+            j = self.half(stream)
             if k == 0:
-                self.x_recv().wait_recv()
-                self.up(1).start()
-                self.down(1).start()
-                self.core(0).start()
+                self.go("wait_recv", z, oxh, c, 0, at(z, oxh, c))
+                self.up("start", 1, 1)
+                self.down("start", 1, 1)
+                self.core("start", 1, 0)
                 return
-            self.up_recv(k).wait_recv()
-            self.down_recv(k).wait_recv()
-            if k < 4:
-                self.up(k + 1).start()
-                self.down(k + 1).start()
-                self.core(2 * k - 1).start()
-                self.core(2 * k).start()
+            if k == 4:
+                self.go("wait_recv", (z + 4) % 8, j, c, 7 * stream + 7, at(zp, xh, c))
+                self.core("start", stream, 7)
+                return
+            self.go("wait_recv", (z + 8 - k) % 8, j, c, 7 * stream + k, at(zp, xh, c))
+            if k < 3:
+                self.up("start", stream, k + 1)
+            self.go("wait_recv", (z + k) % 8, j, c, 7 * stream + 3 + k, at(zm, xh, c))
+            if k < 3:
+                self.down("start", stream, k + 1)
             else:
-                self.core(7).start()
+                self.fourth("start", stream)
+            self.core("start", stream, k)
+            self.core("start", stream, 3 + k)
 
         def end(self):
-            for q in range(8):
-                self.core_recv(q).wait_recv()
+            for stream in range(2):
+                for q in range(8):
+                    self.go("wait_recv", self.unit(q), self.half(stream), oc, 15 + 8 * stream + q, at(z, xh, oc))
 
         def drain(self):
-            self.x_copy().wait_send()
-            for k in range(1, 5):
-                self.up(k).wait_send()
-                self.down(k).wait_send()
-            for q in range(8):
-                self.core(q).wait_send()
-
-    gw = Gather(w_in, wbuf, agw_s, agw_r)
-    gl = Gather(l_in, lbuf, agl_s, agl_r)
+            self.x_copy("wait_send")
+            for stream in range(2):
+                for k in range(1, 4):
+                    self.up("wait_send", stream, k)
+                    self.down("wait_send", stream, k)
+                self.fourth("wait_send", stream)
+                for q in range(8):
+                    self.core("wait_send", stream, q)
+
+    gw = Gather(w_in, wbuf, agw_s, agw_r, False)
+    gl = Gather(l_in, lbuf, agl_s, agl_r, True)
     gw.begin()
-    gl.begin()
 
     ls0 = jnp.full((1, MB), ls_ref[0], F32)
     ls1 = jnp.full((1, MB), ls_ref[1], F32)
@@ -229,7 +238,9 @@
     source = jnp.sum((before <= sub16).astype(jnp.int32), axis=1, keepdims=True) - 1
     source_hot = (lan16 == source).astype(F32)
 
-    gw.step(0)
+    gw.step(0, 1)
+    gw.step(1, 0)
+    gl.begin()
 
     def route_wait(d, carry):
         src = (me + 32 - d) % 32
@@ -273,12 +284,25 @@
             kbuf[rows, lanes] = (jnp.exp2(-(dt * dt + dw * dw)) * mixing).astype(BF16)
         return carry
 
-    for part in range(4):
-        lax.fori_loop(4 * part, 4 * part + 4, cov_block, 0)
-        gw.step(part + 1)
-    gl.step(0)
+    order = (
+        (2, ((gw, 0, 2),)),
+        (4, ((gw, 1, 1),)),
+        (6, ((gl, 0, 1), (gl, 1, 0))),
+        (8, ((gw, 0, 3),)),
+        (10, ((gw, 1, 2), (gl, 0, 2))),
+        (12, ((gw, 0, 4), (gl, 1, 1))),
+        (16, ((gw, 1, 3), (gl, 0, 3), (gw, 1, 4))),
+    )
+    done = 0
+    for upto, events in order:
+        lax.fori_loop(done, upto, cov_block, 0)
+        done = upto
+        for g, stream, k in events:
+            g.step(stream, k)
     gw.end()
 
+    turn = 0
+    plan_l = {3: (1, 2), 6: (0, 4), 9: (1, 3), 13: (1, 4)}
     for part in range(4):
         rows = slice(part * 512, part * 512 + 512)
         for n in range(4):
@@ -290,13 +314,20 @@
                 sq[rows, :] = squares
             else:
                 sq[rows, :] += squares
-        gl.step(part + 1)
+            if turn in plan_l:
+                gl.step(*plan_l[turn])
+            turn += 1
     gl.end()
 
     lane256 = lax.broadcasted_iota(jnp.int32, (256, 128), 1)
-
-    def stat_copy(i):
-        return remote(stats.at[i], gathered.at[ib], st_s.at[i], st_r.at[ib], (me, i))
+    class_ids = lax.broadcasted_iota(jnp.int32, (8, 256), 0)
+    scale = jnp.zeros((8, 256), F32)
+    for n in range(C):
+        scale = jnp.where(class_ids == n, scales_ref[n], scale)
+
+    def term_copy(i, d):
+        slot = terms.at[ib, i]
+        return remote(slot, slot, st_s.at[i, d], st_r.at[i, d], (me, (ib + d) % 8))
 
     def b_block(i, carry):
         rows = pl.ds(pl.multiple_of(i * 256, 256), 256)
@@ -311,16 +342,13 @@
         means = dot_nt(abuf[rows, :], mpad[...])
         var = jnp.sum(squares, axis=1, keepdims=True)
         both = jnp.transpose(jnp.where(lane256 == 8, var, means))
-        stats[i] = both[0:16, :]
-
-        @pl.when(i != ib)
-        def _():
-            stat_copy(i).start()
-
-        @pl.when(i == ib)
-        def _():
-            gathered[ib] = both[0:16, :]
-
+        terms[ib, i] = both[0:8, :] + 0.5 * scale * both[8:9, :]
+
+        def send(d, carry):
+            term_copy(i, d).start()
+            return carry
+
+        lax.fori_loop(1, 8, send, 0)
         return carry
 
     lax.fori_loop(0, 8, b_block, 0)
@@ -330,76 +358,73 @@
         atbuf[:, rows] = jnp.transpose(abuf[rows, :])
         return carry
 
-    lax.fori_loop(0, 3, flip, 0)
-
-    def stat_wait(d, carry):
-        src = (ib + d) % 8
-        remote(stats.at[src], gathered.at[src], st_s.at[src], st_r.at[src], (me, src)).wait_recv()
-        return carry
-
-    lax.fori_loop(1, 8, stat_wait, 0)
-
-    scale = jnp.zeros((8, 256), F32)
-    class_ids = lax.broadcasted_iota(jnp.int32, (8, 256), 0)
-    for n in range(C):
-        scale = jnp.where(class_ids == n, scales_ref[n], scale)
-
-    both = gathered[0]
-    for p in range(1, 8):
-        both = both + gathered[p]
-    band = crow[ib, 1:2, :]
-    own = jnp.zeros((1, 256), F32)
+    lax.fori_loop(0, 8, flip, 0)
+
+    def term_wait(i, carry):
+        def one(d, carry):
+            src = (ib + 8 - d) % 8
+            slot = terms.at[src, i]
+            remote(slot, slot, st_s.at[i, d], st_r.at[i, d], (me, src)).wait_recv()
+            return carry
+
+        return lax.fori_loop(1, 8, one, carry)
+
+    values = []
     for k in range(NB):
         value = jnp.float32(1.0)
         for i in range(NB):
             value = value + mix_ref[k, i] * mix_ref[k, i]
-        own = jnp.where(band == float(k), value, own)
-    logits = both[0:8, :] + 0.5 * scale * (both[8:9, :] + own)
-    weights = jnp.exp(logits)
-    chances = weights / jnp.sum(weights, axis=0, keepdims=True)
-    pieces[ib] = chances
-
-    def piece_copy(d):
-        dev = (ib + d) % 8
-        return remote(pieces.at[ib], pieces.at[ib], pr_s.at[d], pr_r.at[d], (me, dev))
-
-    def piece_start(d, carry):
-        piece_copy(d).start()
-        return carry
-
-    lax.fori_loop(1, 8, piece_start, 0)
-    lax.fori_loop(3, 8, flip, 0)
-
-    def piece_wait(d, carry):
-        src = (ib + 8 - d) % 8
-        remote(pieces.at[src], pieces.at[src], pr_s.at[d], pr_r.at[d], (me, src)).wait_recv()
-        return carry
-
-    lax.fori_loop(1, 8, piece_wait, 0)
-
+        values.append(value)
     classes = class_ids.astype(F32)
-    for p in range(8):
+
+    def likelihood(p):
         lanes = slice(p * 256, p * 256 + 256)
-        ch = pieces[p]
+        logits = terms[0, p]
+        for q in range(1, 8):
+            logits = logits + terms[q, p]
+        band = crow[p, 1:2, :]
+        own = jnp.zeros((1, 256), F32)
+        for k in range(NB):
+            own = jnp.where(band == float(k), values[k], own)
+        weights = jnp.exp(logits + 0.5 * scale * own)
+        ch = weights / jnp.sum(weights, axis=0, keepdims=True)
         probs_out[:, lanes] = ch
         slope = jnp.where(crow[p, 0:1, :] == classes, 1.0, 0.0) - ch
         ms[:, lanes] = jnp.concatenate([slope, jnp.zeros((8, 256), F32)], axis=0).astype(BF16)
-
-    mt0[...] = dot_nn(ms[...], abuf[...])[0:8, :]
+        slope = -jnp.sum(ch * scale, axis=0, keepdims=True)
+        column = jnp.transpose(jnp.broadcast_to(slope, (8, 256)))[:, 0:1]
+        rows = slice(p * 256, p * 256 + 256)
+        hbuf[rows, :] = (column * bbuf[rows, :]).astype(BF16)
+
+    lax.fori_loop(0, 4, term_wait, 0)
+    for p in range(4):
+        likelihood(p)
+    mt0[...] = dot_nn(ms[:, 0:1024], abuf[0:1024, :])[0:8, :]
+    for n in range(4):
+        lanes = slice(n * 256, n * 256 + 256)
+        for lo in range(n * 256, MB, 512):
+            hi = min(lo + 512, MB)
+            bbuf[lo:hi, lanes] = dot_nn(atbuf[lo:hi, 0:1024], hbuf[0:1024, lanes])
+    lax.fori_loop(4, 8, term_wait, 0)
+    for p in range(4, 8):
+        likelihood(p)
+
+    mt0[...] += dot_nn(ms[:, 1024:2048], abuf[1024:2048, :])[0:8, :]
     mean1 = remote(mt0, rm1, m12_s.at[0], m12_r.at[0], at(z, xh, oc))
     mean1.start()
 
-    def h_block(i, carry):
-        rows = pl.ds(pl.multiple_of(i * 256, 256), 256)
-        slope = -jnp.sum(pieces[i] * scale, axis=0, keepdims=True)
-        column = jnp.transpose(jnp.broadcast_to(slope, (8, 256)))[:, 0:1]
-        hbuf[rows, :] = (column * bbuf[rows, :]).astype(BF16)
-        return carry
-
-    lax.fori_loop(0, 8, h_block, 0)
+    colour = xh * 2 + c
 
     def m3_copy(d):
-        return remote(mt2, rm3.at[z], m3_s.at[d], m3_r.at[d], at((z + d) % 8, xh, c))
+        return remote(mt2.at[colour], rm3.at[z], m3_s.at[d], m3_r.at[d], at((z + d) % 8, xh, c))
+
+    def m4_copy(k):
+        dev = (at(z, xh, oc), at(z, oxh, c), at(z, oxh, oc))[k]
+        return remote(quarters.at[colour], quarters.at[colour], m4_s.at[k], m4_r.at[k], dev)
+
+    def m4_recv(k):
+        src = (xh * 2 + oc, oxh * 2 + c, oxh * 2 + oc)[k]
+        return remote(quarters.at[src], quarters.at[src], m4_s.at[k], m4_r.at[k], at(z, xh, oc))
 
     mean2 = remote(mt1, rm2, m12_s.at[1], m12_r.at[1], at(z, oxh, c))
 
@@ -427,8 +452,11 @@
 
     def stage1(n):
         lanes = slice(n * 256, n * 256 + 256)
-        g = dot_nn(atbuf[n * 256 :, :], hbuf[:, lanes]).astype(BF16)
-        gbuf[2 * n :, :, :, :, lanes] = g.reshape(8 - 2 * n, 2, 2, 32, 256)
+        for lo in range(n * 256, MB, 512):
+            hi = min(lo + 512, MB)
+            g = dot_nn(atbuf[lo:hi, 1024:2048], hbuf[1024:2048, lanes])
+            g = (g + bbuf[lo:hi, lanes]).astype(BF16)
+            gbuf[lo // 128 : hi // 128, :, :, :, lanes] = g.reshape((hi - lo) // 128, 2, 2, 32, 256)
         p1_copy(n).start()
 
     def stage2(n):
@@ -463,6 +491,15 @@
             return carry
 
         lax.fori_loop(2 * n, 8, add, 0)
+
+    def m3_start(d, carry):
+        m3_copy(d).start()
+        return carry
+
+    def m3_wait(d, carry):
+        src = (z + 8 - d) % 8
+        remote(mt2.at[colour], rm3.at[src], m3_s.at[d], m3_r.at[d], at(src, xh, c)).wait_recv()
+        return carry
 
     stage1(0)
     mean1.wait_recv()
@@ -470,35 +507,33 @@
     mean2.start()
     stage1(1)
     stage2(0)
-    mean2.wait_recv()
-    mt2[...] = mt1[...] + rm2[...]
-    rm3[z] = mt2[...]
-
-    def m3_start(d, carry):
-        m3_copy(d).start()
-        return carry
-
-    lax.fori_loop(1, 8, m3_start, 0)
     stage1(2)
     stage2(1)
-    stage3(0)
     stage1(3)
     stage2(2)
+    stage2(3)
+    mean2.wait_recv()
+    for k in range(4):
+        lanes = slice(k * 256, k * 256 + 256)
+        mt2[k] = mt1[:, lanes] + rm2[:, lanes]
+    rm3[z] = mt2[colour]
+    lax.fori_loop(1, 8, m3_start, 0)
+    stage3(0)
     stage3(1)
-    stage2(3)
-    stage3(2)
-    stage3(3)
-
-    def m3_wait(d, carry):
-        src = (z + 8 - d) % 8
-        remote(mt2, rm3.at[src], m3_s.at[d], m3_r.at[d], at(src, xh, c)).wait_recv()
-        return carry
-
     lax.fori_loop(1, 8, m3_wait, 0)
     grad = rm3[0]
     for p in range(1, 8):
         grad = grad + rm3[p]
-    gmean_out[...] = grad - m_in[...].astype(F32)
+    quarters[colour] = grad
+    for k in range(3):
+        m4_copy(k).start()
+    stage3(2)
+    stage3(3)
+    for k in range(3):
+        m4_recv(k).wait_recv()
+    for k in range(4):
+        lanes = slice(k * 256, k * 256 + 256)
+        gmean_out[:, lanes] = quarters[k] - m_in[:, lanes].astype(F32)
 
     def p3_wait(n):
         lanes = pl.ds(n * 256, 256)
@@ -537,14 +572,16 @@
     gl.drain()
 
     def ind_drain(d, carry):
-        stat_copy((ib + d) % 8).wait_send()
-        piece_copy(d).wait_send()
+        for i in range(8):
+            term_copy(i, d).wait_send()
         m3_copy(d).wait_send()
         return carry
 
     lax.fori_loop(1, 8, ind_drain, 0)
     mean1.wait_send()
     mean2.wait_send()
+    for k in range(3):
+        m4_copy(k).wait_send()
     for n in range(4):
         p1_copy(n).wait_send()
         p2_copy(n).wait_send()
@@ -592,9 +629,7 @@
             pltpu.VMEM((ROWS, MB), F32),
             pltpu.VMEM((ROWS, MB), BF16),
             pltpu.VMEM((ROWS, 128), F32),
-            pltpu.VMEM((8, 16, 256), F32),
-            pltpu.VMEM((8, 16, 256), F32),
-            pltpu.VMEM((8, 8, 256), F32),
+            pltpu.VMEM((8, 8, 8, 256), F32),
             pltpu.VMEM((16, ROWS), BF16),
             pltpu.VMEM((8, 2, 2, 32, MB), BF16),
             pltpu.VMEM((8, 2, 32, MB), BF16),
@@ -604,14 +639,15 @@
             pltpu.VMEM((8, 32, MB), BF16),
             pltpu.VMEM((8, MB), F32),
             pltpu.VMEM((8, MB), F32),
+            pltpu.VMEM((4, 8, 256), F32),
             pltpu.VMEM((8, MB), F32),
             pltpu.VMEM((8, MB), F32),
-            pltpu.VMEM((8, MB), F32),
-            pltpu.VMEM((8, 8, MB), F32),
-            dma((32,)), dma((32,)), dma((17,)), dma((17,)), dma((17,)), dma((17,)),
-            dma((8,)), dma((8,)), dma((8,)), dma((8,)),
+            pltpu.VMEM((8, 8, 256), F32),
+            pltpu.VMEM((4, 8, 256), F32),
+            dma((32,)), dma((32,)), dma((31,)), dma((31,)), dma((31,)), dma((31,)),
+            dma((8, 8)), dma((8, 8)),
             dma((4,)), dma((4,)), dma((4,)), dma((4,)), dma((4, 8)), dma((4, 8)),
-            dma((2,)), dma((2,)), dma((8,)), dma((8,)),
+            dma((2,)), dma((2,)), dma((8,)), dma((8,)), dma((3,)), dma((3,)),
         ],
         compiler_params=pltpu.CompilerParams(
             collective_id=0, has_side_effects=True, vmem_limit_bytes=60 << 20

time: 99.2 us -> 84.4 us (0.85)
  Pallas kernels: 95.5 us -> 80.6 us
    pallas_call x1, Pallas kernels: 95.5 us -> 80.6 us  [body(): pl.pallas_call(kernel, out_shape=(jax.ShapeDtypeStruct((C, ROWS), F32), j...]
where the time goes in v2:
time: 84.4 us; the launch traced here: 84.2 us
  Pallas kernels  80.6 us (95%)
  local copies, waits for them, and re-layouts  2.88 us (3%)
    pallas_call x1, Pallas kernels, body(): pl.pallas_call(kernel, out_shape=(jax.ShapeDtypeStruct((C, ROWS), F32), j...  80.6 us
    unnamed x7, local copies, waits for them, and re-layouts  2.88 us

profile of v2, /device:TPU:1, one launch (start us, length us, event | category | flops | bytes accessed | tf_op | source)
XLA Modules:
  0.0 84.2 jit_solution(4898351069387005485)
XLA Ops:
  0.6 80.6 %elbo_step.1 = (f32[8,2048]{1,0:T(8,128)}, f32[32,1024]{1,0:T(8,128)}, f32[8,1024]{1,0:T(8,128)}) custom-call(f32[2,4096]{1,0:T(2,128)} %coords_ref.1, s32[32,128]{1,0:T(8,128)} %bitcast.2, s32[32,32]{1,0:T(8,128)} %plan_ref.1, f32[2,1024]{1,0:T(2,128)} %centers_ref.1, s32[8,128]{1,0:T(8,128)} %bitcast.3, f32[6,6]{1,0:T(8,128)} %mix_ref.1, f32[2]{0:T(128)} %ls_ref.1, ...), custom_call_target="tpu_custom_call" | custom-call | tf_op jit(solution)/shard_map/elbo_step/pallas_call | solution.py:606
  81.3 0.0 copy-start
  81.3 1.5 %copy.17 = f32[8,2048]{1,0:T(8,128)} copy(f32[8,2048]{1,0:T(8,128)} %get-tuple-element.6) | data formatting | bytes 131072
  82.8 0.0 copy-done
  82.8 0.0 copy-start.1
  82.8 0.7 copy.18
  83.5 0.1 copy-done.1
  83.6 0.6 copy.19
Async XLA Ops:
  81.3 1.5 %copy-start = (f32[32,1024]{1,0:T(8,128)S(1)}, f32[32,1024]{1,0:T(8,128)}, u32[]{:S(2)}) copy-start(f32[32,1024]{1,0:T(8,128)} %get-tuple-element.7) | copy-start | bytes 393220
  82.8 0.8 copy-start.1

commit v3 on v2

--- a/solution.py
+++ b/solution.py
@@ -31,9 +31,10 @@
 
 
 def kernel(
-    coords_ref, codes_ref, plan_ref, centers_ref, bands_ref, mix_ref, ls_ref, scales_ref,
-    w_in, l_in, m_in,
+    coords_in, codes_in, plan_in, centers_in, bands_in, mix_ref, ls_ref, scales_ref,
+    w_in, l_in, m_any,
     probs_out, gchol_out, gmean_out,
+    coords_ref, codes_ref, plan_ref, centers_ref, bands_ref, m_in, load_sem,
     held, sendbuf, incoming, feat, crow, tab, centers_s, mpad,
     wbuf, lbuf, kbuf, abuf, atbuf, bbuf, hbuf, sq,
     terms, ms,
@@ -61,6 +62,16 @@
             src_ref=src, dst_ref=dst, send_sem=ssem, recv_sem=rsem, device_id=dev, device_id_type=MESH
         )
 
+    loads = [
+        pltpu.make_async_copy(src, dst, load_sem.at[k])
+        for k, (src, dst) in enumerate((
+            (coords_in, coords_ref), (codes_in, codes_ref), (plan_in, plan_ref),
+            (w_in, wbuf.at[z, xh, c]), (l_in, lbuf.at[z, xh, c]),
+            (centers_in, centers_ref), (bands_in, bands_ref), (m_any, m_in),
+        ))
+    ]
+    for copy in loads:
+        copy.start()
     r3[...] = jnp.zeros_like(r3)
 
     barrier = pltpu.get_barrier_semaphore()
@@ -76,6 +87,8 @@
     lax.fori_loop(1, 32, greet_obs, 0)
     lax.fori_loop(1, 8, greet_ind, 0)
 
+    for copy in loads:
+        copy.wait()
     for b in range(32):
         held[0, b : b + 1, :] = coords_ref[0:1, b * 128 : b * 128 + 128]
         held[1, b : b + 1, :] = coords_ref[1:2, b * 128 : b * 128 + 128]
@@ -90,14 +103,12 @@
     sendbuf[:, 2, :] = exact_pick(choose, codes_ref[...].astype(F32))
     sendbuf[:, 3, :] = jnp.zeros((32, 128), F32)
     incoming[me] = sendbuf[me]
-    wbuf[z, xh, c] = w_in[...]
-    lbuf[z, xh, c] = l_in[...]
 
     pl.semaphore_wait(barrier, 38)
 
     def route_copy(d):
         peer = (me + d) % 32
-        return remote(sendbuf.at[peer], incoming.at[me], route_s.at[d], route_r.at[d], (peer, ib))
+        return remote(sendbuf.at[peer], incoming.at[me], route_s, route_r, (peer, ib))
 
     def route_start(d, carry):
         route_copy(d).start()
@@ -106,8 +117,8 @@
     lax.fori_loop(1, 32, route_start, 0)
 
     class Gather:
-        def __init__(self, own, buf, ss, rs, triangular):
-            self.own, self.buf, self.ss, self.rs, self.triangular = own, buf, ss, rs, triangular
+        def __init__(self, buf, ss, rs, triangular):
+            self.buf, self.ss, self.rs, self.triangular = buf, ss, rs, triangular
 
         def widths(self, zz, fn):
             if not self.triangular:
@@ -119,93 +130,100 @@
                 def _():
                     fn(pl.ds(0, (v + 1) * 256))
 
-        def shard(self, zz, j, cc, lanes):
-            if self.triangular:
-                return self.buf.at[zz, j, cc, :, lanes]
-            return self.buf.at[zz, j, cc]
-
-        def go(self, op, zz, j, cc, idx, dev, mine=False):
+        def go(self, op, q, j, cc, idx, dev):
+            zz = self.unit(q)
+
             def fn(lanes):
-                dst = self.shard(zz, j, cc, lanes)
-                src = dst
-                if mine:
-                    src = self.own.at[:, lanes] if self.triangular else self.own
-                copy = remote(src, dst, self.ss.at[idx], self.rs.at[idx], dev)
-                getattr(copy, op)()
+                slot = self.buf.at[zz, j, cc, :, lanes] if self.triangular else self.buf.at[zz, j, cc]
+                getattr(remote(slot, slot, self.ss.at[q], self.rs.at[idx], dev), op)()
 
             self.widths(zz, fn)
+
+        def unit(self, q):
+            return (z + (0, 7, 6, 5, 1, 2, 3, 4)[q]) % 8
 
         def half(self, stream):
             return xh if stream == 0 else oxh
 
-        def up(self, op, stream, k):
-            zz = (z + 8 - (k - 1)) % 8
-            self.go(op, zz, self.half(stream), c, 7 * stream + k, at(zp, xh, c), stream == 0 and k == 1)
-
-        def down(self, op, stream, k):
-            zz = (z + k - 1) % 8
-            self.go(op, zz, self.half(stream), c, 7 * stream + 3 + k, at(zm, xh, c), stream == 0 and k == 1)
-
-        def fourth(self, op, stream):
-            j = self.half(stream)
-            self.go(op, (z + 5 + 6 * j) % 8, j, c, 7 * stream + 7, at((z + 1 + 6 * j) % 8, xh, c))
-
-        def unit(self, q):
-            return (z + (0, 7, 6, 5, 1, 2, 3, 4)[q]) % 8
+        def along(self, op, stream, q, hops, to):
+            idx = 7 * stream + to
+            self.go(op, q, self.half(stream), c, idx, at((z + 8 + hops) % 8, xh, c))
+
+        def fourth(self, op):
+            for j in range(2):
+
+                @pl.when(xh == j)
+                def _():
+                    self.along(op, 0, 3 + 3 * j, 1 - 2 * j, 7)
 
         def core(self, op, stream, q):
-            mine = stream == 0 and q == 0
-            self.go(op, self.unit(q), self.half(stream), c, 15 + 8 * stream + q, at(z, xh, oc), mine)
-
-        def x_copy(self, op):
-            self.go(op, z, xh, c, 0, at(z, oxh, c), True)
+            self.go(op, q, self.half(stream), c, 15, at(z, xh, oc))
+
+        def across(self, op, q):
+            self.go(op, q, xh, c, 7 + q if q else 0, at(z, oxh, c))
+
+        def wait(self, stream, q):
+            idx = 7 * stream + q if q else 0
+            self.go("wait_recv", q, self.half(stream), c, idx, at(z, oxh, c))
 
         def begin(self):
-            self.up("start", 0, 1)
-            self.down("start", 0, 1)
-            self.x_copy("start")
+            self.along("start", 0, 0, 1, 1)
+            self.along("start", 0, 0, -1, 4)
+            self.across("start", 0)
             self.core("start", 0, 0)
 
         def step(self, stream, k):
-            j = self.half(stream)
             if k == 0:
-                self.go("wait_recv", z, oxh, c, 0, at(z, oxh, c))
-                self.up("start", 1, 1)
-                self.down("start", 1, 1)
+                self.wait(1, 0)
+                self.along("start", 1, 0, 1, 1)
+                self.along("start", 1, 0, -1, 4)
                 self.core("start", 1, 0)
                 return
             if k == 4:
-                self.go("wait_recv", (z + 4) % 8, j, c, 7 * stream + 7, at(zp, xh, c))
+                self.wait(stream, 7)
+                if stream == 0:
+                    self.across("start", 7)
                 self.core("start", stream, 7)
                 return
-            self.go("wait_recv", (z + 8 - k) % 8, j, c, 7 * stream + k, at(zp, xh, c))
-            if k < 3:
-                self.up("start", stream, k + 1)
-            self.go("wait_recv", (z + k) % 8, j, c, 7 * stream + 3 + k, at(zm, xh, c))
-            if k < 3:
-                self.down("start", stream, k + 1)
-            else:
-                self.fourth("start", stream)
+            relay = k < 3 - stream
+            self.wait(stream, k)
+            if relay:
+                self.along("start", stream, k, 1, k + 1)
+            self.wait(stream, 3 + k)
+            if relay:
+                self.along("start", stream, 3 + k, -1, 4 + k)
+            if stream == 0 and k == 3:
+                self.fourth("start")
+                self.across("start", 3)
+                self.across("start", 6)
             self.core("start", stream, k)
             self.core("start", stream, 3 + k)
 
         def end(self):
-            for stream in range(2):
-                for q in range(8):
-                    self.go("wait_recv", self.unit(q), self.half(stream), oc, 15 + 8 * stream + q, at(z, xh, oc))
+            rows = pl.ds(0, 320 if self.triangular else 512)
+            remote(kbuf.at[rows], abuf.at[rows], self.ss.at[0], self.rs.at[15], at(z, xh, oc)).wait_recv()
 
         def drain(self):
-            self.x_copy("wait_send")
-            for stream in range(2):
-                for k in range(1, 4):
-                    self.up("wait_send", stream, k)
-                    self.down("wait_send", stream, k)
-                self.fourth("wait_send", stream)
-                for q in range(8):
-                    self.core("wait_send", stream, q)
-
-    gw = Gather(w_in, wbuf, agw_s, agw_r, False)
-    gl = Gather(l_in, lbuf, agl_s, agl_r, True)
+            for q in range(8):
+                many = (7, 4, 3, 3, 4, 3, 3, 3)[q]
+
+                def settle(count):
+                    def fn(lanes):
+                        rows = pl.ds(0, 32 * count)
+                        remote(
+                            kbuf.at[rows, lanes], abuf.at[rows, lanes], self.ss.at[q], self.rs.at[15], at(z, xh, oc)
+                        ).wait_send()
+
+                    self.widths(self.unit(q), fn)
+
+                if q in (3, 6):
+                    pl.when(xh == (q - 3) // 3)(functools.partial(settle, many + 1))
+                    pl.when(xh != (q - 3) // 3)(functools.partial(settle, many))
+                else:
+                    settle(many)
+
+    gw = Gather(wbuf, agw_s, agw_r, False)
+    gl = Gather(lbuf, agl_s, agl_r, True)
     gw.begin()
 
     ls0 = jnp.full((1, MB), ls_ref[0], F32)
@@ -229,7 +247,7 @@
         low = rest - middle
         zeros = jnp.zeros((104, 128), F32)
         tab[:, s * 128 : (s + 1) * 128] = jnp.concatenate([high, middle, low, zeros], axis=0).astype(BF16)
-    mpad[...] = jnp.concatenate([m_in[...].astype(F32), jnp.zeros((120, MB), F32)], axis=0).astype(BF16)
+    mpad[...] = jnp.concatenate([m_in[...].astype(F32), jnp.zeros((8, MB), F32)], axis=0).astype(BF16)
 
     plan_col = jnp.sum(jnp.where(lan == me, plan, 0), axis=1, keepdims=True)
     before = jnp.sum(jnp.where(sub < lan, plan_col, 0), axis=0, keepdims=True)
@@ -242,12 +260,11 @@
     gw.step(1, 0)
     gl.begin()
 
-    def route_wait(d, carry):
-        src = (me + 32 - d) % 32
-        remote(sendbuf.at[src], incoming.at[src], route_s.at[d], route_r.at[d], (src, ib)).wait_recv()
-        return carry
-
-    lax.fori_loop(1, 32, route_wait, 0)
+    def route_all():
+        others = pl.ds(0, 31)
+        return remote(sendbuf.at[others], incoming.at[others], route_s, route_r, ((me + 1) % 32, ib))
+
+    route_all().wait_recv()
 
     st = ROOT / jnp.full((1, 128), ls_ref[0], F32)
     sw = ROOT / jnp.full((1, 128), ls_ref[1], F32)
@@ -290,8 +307,8 @@
         (6, ((gl, 0, 1), (gl, 1, 0))),
         (8, ((gw, 0, 3),)),
         (10, ((gw, 1, 2), (gl, 0, 2))),
-        (12, ((gw, 0, 4), (gl, 1, 1))),
-        (16, ((gw, 1, 3), (gl, 0, 3), (gw, 1, 4))),
+        (13, ((gw, 0, 4), (gl, 1, 1))),
+        (16, ((gl, 0, 3), (gw, 1, 3), (gl, 1, 2), (gw, 1, 4))),
     )
     done = 0
     for upto, events in order:
@@ -302,7 +319,7 @@
     gw.end()
 
     turn = 0
-    plan_l = {3: (1, 2), 6: (0, 4), 9: (1, 3), 13: (1, 4)}
+    plan_l = {3: (0, 4), 9: (1, 3), 13: (1, 4)}
     for part in range(4):
         rows = slice(part * 512, part * 512 + 512)
         for n in range(4):
@@ -317,20 +334,33 @@
             if turn in plan_l:
                 gl.step(*plan_l[turn])
             turn += 1
+    def flip(i, carry):
+        rows = pl.ds(pl.multiple_of(i * 256, 256), 256)
+        atbuf[:, rows] = jnp.transpose(abuf[rows, :])
+        return carry
+
+    lax.fori_loop(0, 4, flip, 0)
     gl.end()
 
-    lane256 = lax.broadcasted_iota(jnp.int32, (256, 128), 1)
     class_ids = lax.broadcasted_iota(jnp.int32, (8, 256), 0)
     scale = jnp.zeros((8, 256), F32)
     for n in range(C):
         scale = jnp.where(class_ids == n, scales_ref[n], scale)
 
+    chunks = ((0, 2), (2, 2), (4, 2), (6, 1), (7, 1))
+
+    def term_slot(src, i):
+        first, many = chunks[i]
+        return terms.at[src, pl.ds(first, many)]
+
     def term_copy(i, d):
-        slot = terms.at[ib, i]
-        return remote(slot, slot, st_s.at[i, d], st_r.at[i, d], (me, (ib + d) % 8))
-
-    def b_block(i, carry):
-        rows = pl.ds(pl.multiple_of(i * 256, 256), 256)
+        slot = term_slot(ib, i)
+        return remote(slot, slot, st_s, st_r.at[i], (me, (ib + d) % 8))
+
+    def b_chunk(i):
+        first, many = chunks[i]
+        lo, size = first * 256, many * 256
+        rows = slice(lo, lo + size)
         squares = -sq[rows, :]
         for n in range(4):
             lanes = slice(n * 256, n * 256 + 256)
@@ -339,35 +369,25 @@
             b = dot_nn(abuf[rows, deep], lower)
             bbuf[rows, lanes] = b
             squares = squares + (b[:, :128] * b[:, :128] + b[:, 128:] * b[:, 128:])
-        means = dot_nt(abuf[rows, :], mpad[...])
-        var = jnp.sum(squares, axis=1, keepdims=True)
-        both = jnp.transpose(jnp.where(lane256 == 8, var, means))
-        terms[ib, i] = both[0:8, :] + 0.5 * scale * both[8:9, :]
+        means = dot_nt(mpad[...], abuf[rows, :])[0:8, :]
+        var = jnp.sum(jnp.transpose(squares), axis=0, keepdims=True)
+        for k in range(many):
+            lanes = slice(k * 256, k * 256 + 256)
+            terms[ib, first + k] = means[:, lanes] + 0.5 * scale * var[:, lanes]
 
         def send(d, carry):
             term_copy(i, d).start()
             return carry
 
         lax.fori_loop(1, 8, send, 0)
-        return carry
-
-    lax.fori_loop(0, 8, b_block, 0)
-
-    def flip(i, carry):
-        rows = pl.ds(pl.multiple_of(i * 256, 256), 256)
-        atbuf[:, rows] = jnp.transpose(abuf[rows, :])
-        return carry
-
-    lax.fori_loop(0, 8, flip, 0)
-
-    def term_wait(i, carry):
-        def one(d, carry):
-            src = (ib + 8 - d) % 8
-            slot = terms.at[src, i]
-            remote(slot, slot, st_s.at[i, d], st_r.at[i, d], (me, src)).wait_recv()
-            return carry
-
-        return lax.fori_loop(1, 8, one, carry)
+
+    for i in range(5):
+        b_chunk(i)
+
+    def term_wait(i):
+        first, many = chunks[i]
+        slot = terms.at[pl.ds(0, 7), pl.ds(first, many)]
+        remote(slot, slot, st_s, st_r.at[i], (me, (ib + 1) % 8)).wait_recv()
 
     values = []
     for k in range(NB):
@@ -396,7 +416,9 @@
         rows = slice(p * 256, p * 256 + 256)
         hbuf[rows, :] = (column * bbuf[rows, :]).astype(BF16)
 
-    lax.fori_loop(0, 4, term_wait, 0)
+    lax.fori_loop(4, 8, flip, 0)
+    term_wait(0)
+    term_wait(1)
     for p in range(4):
         likelihood(p)
     mt0[...] = dot_nn(ms[:, 0:1024], abuf[0:1024, :])[0:8, :]
@@ -405,7 +427,8 @@
         for lo in range(n * 256, MB, 512):
             hi = min(lo + 512, MB)
             bbuf[lo:hi, lanes] = dot_nn(atbuf[lo:hi, 0:1024], hbuf[0:1024, lanes])
-    lax.fori_loop(4, 8, term_wait, 0)
+    for i in range(2, 5):
+        term_wait(i)
     for p in range(4, 8):
         likelihood(p)
 
@@ -416,15 +439,11 @@
     colour = xh * 2 + c
 
     def m3_copy(d):
-        return remote(mt2.at[colour], rm3.at[z], m3_s.at[d], m3_r.at[d], at((z + d) % 8, xh, c))
+        return remote(mt2.at[colour], rm3.at[z], m3_s, m3_r, at((z + d) % 8, xh, c))
 
     def m4_copy(k):
         dev = (at(z, xh, oc), at(z, oxh, c), at(z, oxh, oc))[k]
-        return remote(quarters.at[colour], quarters.at[colour], m4_s.at[k], m4_r.at[k], dev)
-
-    def m4_recv(k):
-        src = (xh * 2 + oc, oxh * 2 + c, oxh * 2 + oc)[k]
-        return remote(quarters.at[src], quarters.at[src], m4_s.at[k], m4_r.at[k], at(z, xh, oc))
+        return remote(quarters.at[colour], quarters.at[colour], m4_s, m4_r, dev)
 
     mean2 = remote(mt1, rm2, m12_s.at[1], m12_r.at[1], at(z, oxh, c))
 
@@ -447,7 +466,7 @@
     def p3_copy(n, zz):
         lanes = pl.ds(n * 256, 256)
         return remote(
-            s2.at[zz, :, lanes], r3.at[z, :, lanes], p3_s.at[n, zz], p3_r.at[n, z], at(zz, xh, c)
+            s2.at[zz, :, lanes], r3.at[z, :, lanes], p3_s.at[n], p3_r.at[n], at(zz, xh, c)
         )
 
     def stage1(n):
@@ -496,10 +515,11 @@
         m3_copy(d).start()
         return carry
 
-    def m3_wait(d, carry):
-        src = (z + 8 - d) % 8
-        remote(mt2.at[colour], rm3.at[src], m3_s.at[d], m3_r.at[d], at(src, xh, c)).wait_recv()
-        return carry
+    def m3_all():
+        return remote(rm3.at[pl.ds(0, 7)], rm3.at[pl.ds(0, 7)], m3_s, m3_r, at(zp, xh, c))
+
+    def m4_all():
+        return remote(quarters.at[pl.ds(0, 3)], quarters.at[pl.ds(0, 3)], m4_s, m4_r, at(z, xh, oc))
 
     stage1(0)
     mean1.wait_recv()
@@ -520,7 +540,7 @@
     lax.fori_loop(1, 8, m3_start, 0)
     stage3(0)
     stage3(1)
-    lax.fori_loop(1, 8, m3_wait, 0)
+    m3_all().wait_recv()
     grad = rm3[0]
     for p in range(1, 8):
         grad = grad + rm3[p]
@@ -529,25 +549,21 @@
         m4_copy(k).start()
     stage3(2)
     stage3(3)
-    for k in range(3):
-        m4_recv(k).wait_recv()
+    m4_all().wait_recv()
     for k in range(4):
         lanes = slice(k * 256, k * 256 + 256)
         gmean_out[:, lanes] = quarters[k] - m_in[:, lanes].astype(F32)
 
+    def p3_all(n, many):
+        lanes = pl.ds(n * 256, 256)
+        return remote(
+            s2.at[pl.ds(0, many), :, lanes], r3.at[pl.ds(0, many), :, lanes], p3_s.at[n], p3_r.at[n], at(zp, xh, c)
+        )
+
     def p3_wait(n):
-        lanes = pl.ds(n * 256, 256)
-
-        def one(d, carry):
-            src = (z + 8 - d) % 8
-            remote(
-                s2.at[src, :, lanes], r3.at[src, :, lanes], p3_s.at[n, src], p3_r.at[n, src], at(src, xh, c)
-            ).wait_recv()
-            return carry
-
         @pl.when(z >= 2 * n)
         def _():
-            lax.fori_loop(1, 8, one, 0)
+            p3_all(n, 7).wait_recv()
 
     for n in range(4):
         p3_wait(n)
@@ -556,44 +572,34 @@
         data = data + r3[p].astype(F32)
     column_ids = lax.broadcasted_iota(jnp.int32, (32, MB), 1)
     row_ids = lax.broadcasted_iota(jnp.int32, (32, MB), 0) + me * 32
-    own_chol = l_in[...].astype(F32)
+    own_chol = lbuf[z, xh, c].astype(F32)
     on_diag = column_ids == row_ids
     diagonal = jnp.sum(jnp.where(on_diag, own_chol, 0.0), axis=1, keepdims=True)
     gchol_out[...] = (
         jnp.where(column_ids <= row_ids, data, 0.0) - own_chol + jnp.where(on_diag, 1.0 / diagonal, 0.0)
     )
 
-    def route_drain(d, carry):
-        route_copy(d).wait_send()
-        return carry
-
-    lax.fori_loop(1, 32, route_drain, 0)
+    route_all().wait_send()
     gw.drain()
     gl.drain()
 
-    def ind_drain(d, carry):
-        for i in range(8):
-            term_copy(i, d).wait_send()
-        m3_copy(d).wait_send()
-        return carry
-
-    lax.fori_loop(1, 8, ind_drain, 0)
+    slot = terms.at[pl.ds(0, 7)]
+    remote(slot, slot, st_s, st_r.at[0], (me, (ib + 1) % 8)).wait_send()
     mean1.wait_send()
     mean2.wait_send()
-    for k in range(3):
-        m4_copy(k).wait_send()
+    m3_all().wait_send()
+    m4_all().wait_send()
     for n in range(4):
         p1_copy(n).wait_send()
         p2_copy(n).wait_send()
 
-        def p3_drain(zz, carry):
-            @pl.when(zz != z)
-            def _():
-                p3_copy(n, zz).wait_send()
-
-            return carry
-
-        lax.fori_loop(2 * n, 8, p3_drain, 0)
+        @pl.when(z >= 2 * n)
+        def _():
+            p3_all(n, 7 - 2 * n).wait_send()
+
+        @pl.when(z < 2 * n)
+        def _():
+            p3_all(n, 8 - 2 * n).wait_send()
 
 
 def body(
@@ -601,18 +607,26 @@
     class_scales, prior_factor, variational_chol, variational_mean,
 ):
     vmem = pl.BlockSpec(memory_space=pltpu.VMEM)
+    whole = pl.BlockSpec(memory_space=pl.ANY)
     smem = pl.BlockSpec(memory_space=pltpu.SMEM)
     dma = pltpu.SemaphoreType.DMA
     return pl.pallas_call(
         kernel,
         out_shape=(
-            jax.ShapeDtypeStruct((C, ROWS), F32),
-            jax.ShapeDtypeStruct((32, MB), F32),
-            jax.ShapeDtypeStruct((C, MB), F32),
+            pltpu.VMEM((C, ROWS), F32),
+            pltpu.VMEM((32, MB), F32),
+            pltpu.VMEM((C, MB), F32),
         ),
-        in_specs=[vmem, vmem, vmem, vmem, vmem, smem, smem, smem, vmem, vmem, vmem],
+        in_specs=[whole] * 5 + [smem] * 3 + [whole] * 3,
         out_specs=(vmem, vmem, vmem),
         scratch_shapes=[
+            pltpu.VMEM((2, 4096), F32),
+            pltpu.VMEM((32, 128), jnp.int32),
+            pltpu.VMEM((32, 32), jnp.int32),
+            pltpu.VMEM((2, MB), F32),
+            pltpu.VMEM((8, 128), jnp.int32),
+            pltpu.VMEM((C, MB), BF16),
+            dma((8,)),
             pltpu.VMEM((2, 32, 128), F32),
             pltpu.VMEM((32, 4, 128), F32),
             pltpu.VMEM((32, 4, 128), F32),
@@ -620,7 +634,7 @@
             pltpu.VMEM((8, 2, 256), F32),
             pltpu.VMEM((128, MB), BF16),
             pltpu.VMEM((2, MB), F32),
-            pltpu.VMEM((128, MB), BF16),
+            pltpu.VMEM((16, MB), BF16),
             pltpu.VMEM((8, 2, 2, 32, MB), BF16),
             pltpu.VMEM((8, 2, 2, 32, MB), BF16),
             pltpu.VMEM((ROWS, MB), BF16),
@@ -644,10 +658,10 @@
             pltpu.VMEM((8, MB), F32),
             pltpu.VMEM((8, 8, 256), F32),
             pltpu.VMEM((4, 8, 256), F32),
-            dma((32,)), dma((32,)), dma((31,)), dma((31,)), dma((31,)), dma((31,)),
-            dma((8, 8)), dma((8, 8)),
-            dma((4,)), dma((4,)), dma((4,)), dma((4,)), dma((4, 8)), dma((4, 8)),
-            dma((2,)), dma((2,)), dma((8,)), dma((8,)), dma((3,)), dma((3,)),
+            dma(()), dma(()), dma((8,)), dma((16,)), dma((8,)), dma((16,)),
+            dma(()), dma((5,)),
+            dma((4,)), dma((4,)), dma((4,)), dma((4,)), dma((4,)), dma((4,)),
+            dma((2,)), dma((2,)), dma(()), dma(()), dma(()), dma(()),
         ],
         compiler_params=pltpu.CompilerParams(
             collective_id=0, has_side_effects=True, vmem_limit_bytes=60 << 20

time: 84.4 us -> 75.2 us (0.89)
  Pallas kernels: 80.6 us -> 72.5 us
  local copies, waits for them, and re-layouts: 2.88 us -> 1.9 us
    pallas_call x1, Pallas kernels: 80.6 us -> 72.5 us  [body(): pl.pallas_call(kernel, out_shape=(pltpu.VMEM((C, ROWS), F32), pltpu.VMEM(...]
    unnamed x7 -> x3, local copies, waits for them, and re-layouts: 2.88 us -> 1.9 us
where the time goes in v3:
time: 75.2 us; the launch traced here: 75 us
  Pallas kernels  72.5 us (96%)
  local copies, waits for them, and re-layouts  1.9 us (3%)
    pallas_call x1, Pallas kernels, body(): pl.pallas_call(kernel, out_shape=(pltpu.VMEM((C, ROWS), F32), pltpu.VMEM(...  72.5 us
    unnamed x3, local copies, waits for them, and re-layouts  1.9 us

profile of v3, /device:TPU:1, one launch (start us, length us, event | category | flops | bytes accessed | tf_op | source)
XLA Modules:
  0.0 75.0 jit_solution(12601612434185275369)
XLA Ops:
  0.6 72.5 %elbo_step.1 = (f32[8,2048]{1,0:T(8,128)S(1)}, f32[32,1024]{1,0:T(8,128)S(1)}, f32[8,1024]{1,0:T(8,128)S(1)}) custom-call(f32[2,4096]{1,0:T(2,128)} %coords_in.1, s32[32,128]{1,0:T(8,128)} %bitcast.2, s32[32,32]{1,0:T(8,128)} %plan_in.1, f32[2,1024]{1,0:T(2,128)} %centers_in.1, s32[8,128]{1,0:T(8,128)} %bitcast.3, f32[6,6]{1,0:T(8,128)} %mix_ref.1, ...), custom_call_target="tpu_custom_call" | custom-call | tf_op jit(solution)/shard_map/elbo_step/pallas_call | solution.py:613
  73.1 0.6 copy.17
  73.7 0.6 copy.19
  74.3 0.7 copy.18

commit v4 on v3

--- a/solution.py
+++ b/solution.py
@@ -113,8 +113,6 @@
     def route_start(d, carry):
         route_copy(d).start()
         return carry
-
-    lax.fori_loop(1, 32, route_start, 0)
 
     class Gather:
         def __init__(self, buf, ss, rs, triangular):
@@ -225,6 +223,7 @@
     gw = Gather(wbuf, agw_s, agw_r, False)
     gl = Gather(lbuf, agl_s, agl_r, True)
     gw.begin()
+    lax.fori_loop(1, 32, route_start, 0)
 
     ls0 = jnp.full((1, MB), ls_ref[0], F32)
     ls1 = jnp.full((1, MB), ls_ref[1], F32)
@@ -308,7 +307,7 @@
         (8, ((gw, 0, 3),)),
         (10, ((gw, 1, 2), (gl, 0, 2))),
         (13, ((gw, 0, 4), (gl, 1, 1))),
-        (16, ((gl, 0, 3), (gw, 1, 3), (gl, 1, 2), (gw, 1, 4))),
+        (16, ((gw, 1, 3), (gl, 0, 3), (gw, 1, 4), (gl, 1, 2))),
     )
     done = 0
     for upto, events in order:
@@ -495,21 +494,26 @@
         p2_copy(n).wait_recv()
         lanes = pl.ds(n * 256, 256)
 
-        def add(zz, carry):
-            total = s1[zz, xh, :, lanes].astype(F32) + r2[zz, :, lanes].astype(F32)
-            s2[zz, :, lanes] = total.astype(BF16)
-
-            @pl.when(zz != z)
+        def add(d, carry):
+            odd = d % 2
+            zz = (z + 4 + (d // 2) * (1 - odd) + (8 - (d + 1) // 2) * odd) % 8
+
+            @pl.when(zz >= 2 * n)
             def _():
-                p3_copy(n, zz).start()
-
-            @pl.when(zz == z)
-            def _():
-                r3[z, :, lanes] = total.astype(BF16)
+                total = s1[zz, xh, :, lanes].astype(F32) + r2[zz, :, lanes].astype(F32)
+                s2[zz, :, lanes] = total.astype(BF16)
+
+                @pl.when(zz != z)
+                def _():
+                    p3_copy(n, zz).start()
+
+                @pl.when(zz == z)
+                def _():
+                    r3[z, :, lanes] = total.astype(BF16)
 
             return carry
 
-        lax.fori_loop(2 * n, 8, add, 0)
+        lax.fori_loop(0, 8, add, 0)
 
     def m3_start(d, carry):
         m3_copy(d).start()
@@ -521,25 +525,27 @@
     def m4_all():
         return remote(quarters.at[pl.ds(0, 3)], quarters.at[pl.ds(0, 3)], m4_s, m4_r, at(z, xh, oc))
 
-    stage1(0)
+    stage1(3)
+    stage1(2)
     mean1.wait_recv()
     mt1[...] = mt0[...] + rm1[...]
     mean2.start()
+    stage2(3)
     stage1(1)
-    stage2(0)
-    stage1(2)
+    stage2(2)
+    stage1(0)
     stage2(1)
-    stage1(3)
-    stage2(2)
-    stage2(3)
     mean2.wait_recv()
     for k in range(4):
         lanes = slice(k * 256, k * 256 + 256)
         mt2[k] = mt1[:, lanes] + rm2[:, lanes]
     rm3[z] = mt2[colour]
     lax.fori_loop(1, 8, m3_start, 0)
+    stage2(0)
+    stage3(3)
+    stage3(2)
+    stage3(1)
     stage3(0)
-    stage3(1)
     m3_all().wait_recv()
     grad = rm3[0]
     for p in range(1, 8):
@@ -547,8 +553,6 @@
     quarters[colour] = grad
     for k in range(3):
         m4_copy(k).start()
-    stage3(2)
-    stage3(3)
     m4_all().wait_recv()
     for k in range(4):
         lanes = slice(k * 256, k * 256 + 256)

time: 75.2 us -> 72.8 us (0.968)
  Pallas kernels: 72.5 us -> 70.1 us
    pallas_call x1, Pallas kernels: 72.5 us -> 70.1 us  [body(): pl.pallas_call(kernel, out_shape=(pltpu.VMEM((C, ROWS), F32), pltpu.VMEM(...]
where the time goes in v4:
time: 72.8 us; the launch traced here: 72.7 us
  Pallas kernels  70.1 us (96%)
  local copies, waits for them, and re-layouts  1.9 us (3%)
    pallas_call x1, Pallas kernels, body(): pl.pallas_call(kernel, out_shape=(pltpu.VMEM((C, ROWS), F32), pltpu.VMEM(...  70.1 us
    unnamed x3, local copies, waits for them, and re-layouts  1.9 us

profile of v4, /device:TPU:1, one launch (start us, length us, event | category | flops | bytes accessed | tf_op | source)
XLA Modules:
  0.0 72.7 jit_solution(7744062116702371583)
XLA Ops:
  0.6 70.1 %elbo_step.1 = (f32[8,2048]{1,0:T(8,128)S(1)}, f32[32,1024]{1,0:T(8,128)S(1)}, f32[8,1024]{1,0:T(8,128)S(1)}) custom-call(f32[2,4096]{1,0:T(2,128)} %coords_in.1, s32[32,128]{1,0:T(8,128)} %bitcast.2, s32[32,32]{1,0:T(8,128)} %plan_in.1, f32[2,1024]{1,0:T(2,128)} %centers_in.1, s32[8,128]{1,0:T(8,128)} %bitcast.3, f32[6,6]{1,0:T(8,128)} %mix_ref.1, ...), custom_call_target="tpu_custom_call" | custom-call | tf_op jit(solution)/shard_map/elbo_step/pallas_call | solution.py:617
  70.7 0.6 copy.17
  71.4 0.6 copy.19
  72.0 0.7 copy.18

commit v5 on v4

--- a/solution.py
+++ b/solution.py
@@ -31,10 +31,10 @@
 
 
 def kernel(
-    coords_in, codes_in, plan_in, centers_in, bands_in, mix_ref, ls_ref, scales_ref,
+    coords_in, codes_in, plan_in, centers_in, bands_in, mix_in, ls_in, scales_in,
     w_in, l_in, m_any,
     probs_out, gchol_out, gmean_out,
-    coords_ref, codes_ref, plan_ref, centers_ref, bands_ref, m_in, load_sem,
+    coords_ref, codes_ref, plan_ref, centers_ref, bands_ref, m_in, mix_ref, ls_ref, scales_ref, load_sem,
     held, sendbuf, incoming, feat, crow, tab, centers_s, mpad,
     wbuf, lbuf, kbuf, abuf, atbuf, bbuf, hbuf, sq,
     terms, ms,
@@ -68,6 +68,7 @@
             (coords_in, coords_ref), (codes_in, codes_ref), (plan_in, plan_ref),
             (w_in, wbuf.at[z, xh, c]), (l_in, lbuf.at[z, xh, c]),
             (centers_in, centers_ref), (bands_in, bands_ref), (m_any, m_in),
+            (mix_in, mix_ref), (ls_in, ls_ref), (scales_in, scales_ref),
         ))
     ]
     for copy in loads:
@@ -338,7 +339,6 @@
         atbuf[:, rows] = jnp.transpose(abuf[rows, :])
         return carry
 
-    lax.fori_loop(0, 4, flip, 0)
     gl.end()
 
     class_ids = lax.broadcasted_iota(jnp.int32, (8, 256), 0)
@@ -415,7 +415,7 @@
         rows = slice(p * 256, p * 256 + 256)
         hbuf[rows, :] = (column * bbuf[rows, :]).astype(BF16)
 
-    lax.fori_loop(4, 8, flip, 0)
+    lax.fori_loop(0, 8, flip, 0)
     term_wait(0)
     term_wait(1)
     for p in range(4):
@@ -612,7 +612,6 @@
 ):
     vmem = pl.BlockSpec(memory_space=pltpu.VMEM)
     whole = pl.BlockSpec(memory_space=pl.ANY)
-    smem = pl.BlockSpec(memory_space=pltpu.SMEM)
     dma = pltpu.SemaphoreType.DMA
     return pl.pallas_call(
         kernel,
@@ -621,7 +620,7 @@
             pltpu.VMEM((32, MB), F32),
             pltpu.VMEM((C, MB), F32),
         ),
-        in_specs=[whole] * 5 + [smem] * 3 + [whole] * 3,
+        in_specs=[whole] * 11,
         out_specs=(vmem, vmem, vmem),
         scratch_shapes=[
             pltpu.VMEM((2, 4096), F32),
@@ -630,7 +629,8 @@
             pltpu.VMEM((2, MB), F32),
             pltpu.VMEM((8, 128), jnp.int32),
             pltpu.VMEM((C, MB), BF16),
-            dma((8,)),
+            pltpu.SMEM((NB, NB), F32), pltpu.SMEM((2,), F32), pltpu.SMEM((C,), F32),
+            dma((11,)),
             pltpu.VMEM((2, 32, 128), F32),
             pltpu.VMEM((32, 4, 128), F32),
             pltpu.VMEM((32, 4, 128), F32),

time: 72.8 us -> 71.4 us (0.981)
  Pallas kernels: 70.1 us -> 68.8 us
    pallas_call x1, Pallas kernels: 70.1 us -> 68.8 us  [body(): pl.pallas_call(kernel, out_shape=(pltpu.VMEM((C, ROWS), F32), pltpu.VMEM(...]
where the time goes in v5:
time: 71.4 us; the launch traced here: 71.3 us
  Pallas kernels  68.8 us (96%)
  local copies, waits for them, and re-layouts  1.9 us (3%)
    pallas_call x1, Pallas kernels, body(): pl.pallas_call(kernel, out_shape=(pltpu.VMEM((C, ROWS), F32), pltpu.VMEM(...  68.8 us
    unnamed x3, local copies, waits for them, and re-layouts  1.9 us

profile of v5, /device:TPU:1, one launch (start us, length us, event | category | flops | bytes accessed | tf_op | source)
XLA Modules:
  0.0 71.3 jit_solution(5965099288174314833)
XLA Ops:
  0.6 68.8 %elbo_step.1 = (f32[8,2048]{1,0:T(8,128)S(1)}, f32[32,1024]{1,0:T(8,128)S(1)}, f32[8,1024]{1,0:T(8,128)S(1)}) custom-call(f32[2,4096]{1,0:T(2,128)} %coords_in.1, s32[32,128]{1,0:T(8,128)} %bitcast.2, s32[32,32]{1,0:T(8,128)} %plan_in.1, f32[2,1024]{1,0:T(2,128)} %centers_in.1, s32[8,128]{1,0:T(8,128)} %bitcast.3, f32[6,6]{1,0:T(8,128)} %mix_in.1, f32[2]{0:T(128)} %ls_in.1, ...), custom_call_target="tpu_custom_call" | custom-call | tf_op jit(solution)/shard_map/elbo_step/pallas_call | solution.py:616
  69.4 0.6 copy.17
  70.0 0.6 copy.19
  70.6 0.7 copy.18

commit v6 on v5

--- a/solution.py
+++ b/solution.py
@@ -454,16 +454,19 @@
             p1_s.at[n], p1_r.at[n], at(z, xh, oc),
         )
 
+    parts = ((0, 128), (256, 256), (512, 256), (768, 256), (128, 128))
+    firsts = (0, 2, 4, 6, 0)
+
     def p2_copy(n):
-        lanes = pl.ds(n * 256, 256)
+        lanes = pl.ds(*parts[n])
         return remote(
-            s1.at[pl.ds(2 * n, 8 - 2 * n), oxh, :, lanes],
-            r2.at[pl.ds(2 * n, 8 - 2 * n), :, lanes],
+            s1.at[pl.ds(firsts[n], 8 - firsts[n]), oxh, :, lanes],
+            r2.at[pl.ds(firsts[n], 8 - firsts[n]), :, lanes],
             p2_s.at[n], p2_r.at[n], at(z, oxh, c),
         )
 
     def p3_copy(n, zz):
-        lanes = pl.ds(n * 256, 256)
+        lanes = pl.ds(*parts[n])
         return remote(
             s2.at[zz, :, lanes], r3.at[z, :, lanes], p3_s.at[n], p3_r.at[n], at(zz, xh, c)
         )
@@ -479,26 +482,27 @@
 
     def stage2(n):
         p1_copy(n).wait_recv()
-        lanes = pl.ds(n * 256, 256)
-
-        def add(zz, carry):
-            for j in range(2):
-                total = gbuf[zz, j, c, :, lanes].astype(F32) + r1[zz, j, :, lanes].astype(F32)
-                s1[zz, j, :, lanes] = total.astype(BF16)
-            return carry
-
-        lax.fori_loop(2 * n, 8, add, 0)
-        p2_copy(n).start()
+        for part in (0, 4) if n == 0 else (n,):
+            lanes = pl.ds(*parts[part])
+
+            def add(zz, carry):
+                for j in range(2):
+                    total = gbuf[zz, j, c, :, lanes].astype(F32) + r1[zz, j, :, lanes].astype(F32)
+                    s1[zz, j, :, lanes] = total.astype(BF16)
+                return carry
+
+            lax.fori_loop(2 * n, 8, add, 0)
+            p2_copy(part).start()
 
     def stage3(n):
         p2_copy(n).wait_recv()
-        lanes = pl.ds(n * 256, 256)
+        lanes = pl.ds(*parts[n])
 
         def add(d, carry):
             odd = d % 2
             zz = (z + 4 + (d // 2) * (1 - odd) + (8 - (d + 1) // 2) * odd) % 8
 
-            @pl.when(zz >= 2 * n)
+            @pl.when(zz >= firsts[n])
             def _():
                 total = s1[zz, xh, :, lanes].astype(F32) + r2[zz, :, lanes].astype(F32)
                 s2[zz, :, lanes] = total.astype(BF16)
@@ -546,6 +550,7 @@
     stage3(2)
     stage3(1)
     stage3(0)
+    stage3(4)
     m3_all().wait_recv()
     grad = rm3[0]
     for p in range(1, 8):
@@ -559,17 +564,17 @@
         gmean_out[:, lanes] = quarters[k] - m_in[:, lanes].astype(F32)
 
     def p3_all(n, many):
-        lanes = pl.ds(n * 256, 256)
+        lanes = pl.ds(*parts[n])
         return remote(
             s2.at[pl.ds(0, many), :, lanes], r3.at[pl.ds(0, many), :, lanes], p3_s.at[n], p3_r.at[n], at(zp, xh, c)
         )
 
     def p3_wait(n):
-        @pl.when(z >= 2 * n)
+        @pl.when(z >= firsts[n])
         def _():
             p3_all(n, 7).wait_recv()
 
-    for n in range(4):
+    for n in range(5):
         p3_wait(n)
     data = r3[0].astype(F32)
     for p in range(1, 8):
@@ -595,15 +600,16 @@
     m4_all().wait_send()
     for n in range(4):
         p1_copy(n).wait_send()
+    for n in range(5):
         p2_copy(n).wait_send()
 
-        @pl.when(z >= 2 * n)
+        @pl.when(z >= firsts[n])
         def _():
-            p3_all(n, 7 - 2 * n).wait_send()
-
-        @pl.when(z < 2 * n)
+            p3_all(n, 7 - firsts[n]).wait_send()
+
+        @pl.when(z < firsts[n])
         def _():
-            p3_all(n, 8 - 2 * n).wait_send()
+            p3_all(n, 8 - firsts[n]).wait_send()
 
 
 def body(
@@ -664,7 +670,7 @@
             pltpu.VMEM((4, 8, 256), F32),
             dma(()), dma(()), dma((8,)), dma((16,)), dma((8,)), dma((16,)),
             dma(()), dma((5,)),
-            dma((4,)), dma((4,)), dma((4,)), dma((4,)), dma((4,)), dma((4,)),
+            dma((4,)), dma((4,)), dma((5,)), dma((5,)), dma((5,)), dma((5,)),
             dma((2,)), dma((2,)), dma(()), dma(()), dma(()), dma(()),
         ],
         compiler_params=pltpu.CompilerParams(

time: 71.4 us -> 71.7 us (level)
  no operation moved by 1% of the time
where the time goes in v6:
time: 71.7 us; the launch traced here: 71.6 us
  Pallas kernels  69.1 us (96%)
  local copies, waits for them, and re-layouts  1.9 us (3%)
    pallas_call x1, Pallas kernels, body(): pl.pallas_call(kernel, out_shape=(pltpu.VMEM((C, ROWS), F32), pltpu.VMEM(...  69.1 us
    unnamed x3, local copies, waits for them, and re-layouts  1.9 us

profile of v6, /device:TPU:1, one launch (start us, length us, event | category | flops | bytes accessed | tf_op | source)
XLA Modules:
  0.0 71.6 jit_solution(11516656125055957872)
XLA Ops:
  0.6 69.1 %elbo_step.1 = (f32[8,2048]{1,0:T(8,128)S(1)}, f32[32,1024]{1,0:T(8,128)S(1)}, f32[8,1024]{1,0:T(8,128)S(1)}) custom-call(f32[2,4096]{1,0:T(2,128)} %coords_in.1, s32[32,128]{1,0:T(8,128)} %bitcast.2, s32[32,32]{1,0:T(8,128)} %plan_in.1, f32[2,1024]{1,0:T(2,128)} %centers_in.1, s32[8,128]{1,0:T(8,128)} %bitcast.3, f32[6,6]{1,0:T(8,128)} %mix_in.1, f32[2]{0:T(128)} %ls_in.1, ...), custom_call_target="tpu_custom_call" | custom-call | tf_op jit(solution)/shard_map/elbo_step/pallas_call | solution.py:622
  69.7 0.6 copy.17
  70.3 0.6 copy.19
  70.9 0.7 copy.18
